TPU v7x, 32 devices: a whole 2x2x4 slice. The times are simulated.
32 devices in a mesh: comp: 4 (over y, core), dom: 8 (over z, x).
Axes of the slice: x: 2, y: 2, z: 4, core: 2. Of those that a mesh axis runs over, the one named last changes fastest.
Arguments:
- source_field: bfloat16 [4, 8, 32, 16, 128], P('comp', 'dom'), may hold values from -108 to 108, as said below
- source_block: int32 [4, 8, 12], P('comp', 'dom'), may hold values from 0 to 31
- margin: int32 [4, 8, 12, 2], P('comp', 'dom'), may hold values from 0 to 31, as said below
- remap_weight: bfloat16 [4, 8, 12, 128, 128], P('comp', 'dom'), may hold values from 0 to 0.7, as said below
- helm_coef: float32 [256, 512], P('dom', 'comp'), may hold values from 0.05 to 1
Outputs:
- solution: float32 [16, 256, 512], P(None, 'dom', 'comp')
- residual: float32 [16, 256, 512], P(None, 'dom', 'comp')
Inputs may be any that keep to these rules, and one draw needn't show every extreme that they name: `source_field`: each value is a normal or uniform draw times scales that vary by field level, cell and device. `margin`: for each device and each owner, at most 4 of the device's entries name that owner and they name at most 2 distinct target rows; on every device some owner has exactly 4 entries. `remap_weight`: Nonnegative.
All inputs are finite; a program needn't handle non-finite values.
Results may differ from a plain program's by a relative error of at most 0.0003.
Values sent between devices are 32-bit elements; how exact they have to be, the bound alone decides.
No kernel may reach another device: no remote copies, remote signals or barrier semaphores. Data moves between devices by JAX's collectives and lax.ppermute only.
A program may use at most 64 MiB of HBM per device.

v0:
```python
import jax
import jax.numpy as jnp
from jax import lax
from jax.sharding import PartitionSpec as P

CAP = 4
ITERS = 2


HIGHEST = lax.Precision.HIGHEST


def with_halo(array, sides, width):
    for axis, dim in sides:
        devices, length = (lax.axis_size(axis), array.shape[dim])
        up = [(i, (i + 1) % devices) for i in range(devices - 1)]
        down = [(j, i) for i, j in up]
        last = lax.slice_in_dim(array, length - width, length, axis=dim)
        initial = lax.slice_in_dim(array, 0, width, axis=dim)
        before = lax.ppermute(last, axis, up)
        after = lax.ppermute(initial, axis, down)
        array = jnp.concatenate([before, array, after], axis=dim)
    return array


def row_dots(left, right):
    return jnp.sum(left * right, axis=(1, 2))


def operate(current, helm_coef):
    padded = with_halo(current, (("comp", 2), ("dom", 1)), 1)
    beside = padded[:, 2:, 1:-1] + padded[:, :-2, 1:-1] + padded[:, 1:-1, 2:] + padded[:, 1:-1, :-2]
    return (4.0 + helm_coef) * current - beside


def two_products(residual, applied):
    return lax.psum((row_dots(residual, residual), row_dots(residual, applied)), ("comp", "dom"))


def per_device(source_field, source_block, margin, remap_weight, helm_coef):
    sources = source_field[0, 0]
    block_ids = source_block[0, 0]
    peer_ids = margin[0, 0, :, 0]
    row_dest = margin[0, 0, :, 1]
    weights = remap_weight[0, 0]
    picked = jnp.take(sources, block_ids, axis=0)
    remapped = jnp.einsum("krs,kts->krt", picked, weights, preferred_element_type=jnp.float32)
    groups = lax.axis_size("comp")
    entries = peer_ids.shape[0]
    rows_here = helm_coef.shape[0]
    position = jnp.arange(entries, dtype=jnp.int32)
    earlier = position[None, :] < position[:, None]
    same_peer = peer_ids[:, None] == peer_ids[None, :]
    slot_ids = jnp.sum(earlier & same_peer, axis=1)
    slot_width = CAP
    slot_total = groups * slot_width
    placing = (
        (peer_ids * slot_width + slot_ids)[:, None]
        == jnp.arange(slot_total, dtype=jnp.int32)[None, :]
    ).astype(jnp.float32)
    outgoing = jnp.einsum("ks,krb->srb", placing, remapped, precision=HIGHEST)
    labels = jnp.max(placing * (row_dest + 1).astype(jnp.float32)[:, None], axis=0) - 1.0
    arrived, arrived_labels = (
        lax.all_to_all(outgoing, "comp", split_axis=0, concat_axis=0, tiled=True),
        lax.all_to_all(labels, "comp", split_axis=0, concat_axis=0, tiled=True),
    )
    landing = (
        arrived_labels.astype(jnp.int32)[:, None] == jnp.arange(rows_here, dtype=jnp.int32)[None, :]
    ).astype(jnp.float32)
    target = jnp.einsum("st,srb->rtb", landing, arrived, precision=HIGHEST)
    solution = jnp.zeros_like(target)
    residual = target
    applied = operate(residual, helm_coef)
    norm_now, product = two_products(residual, applied)
    step_len = norm_now / product
    direction = residual
    along = applied
    for step in range(ITERS):
        solution = solution + step_len[:, None, None] * direction
        residual = residual - step_len[:, None, None] * along
        if step + 1 < ITERS:
            applied = operate(residual, helm_coef)
            norm_next, product = two_products(residual, applied)
            ratio = norm_next / norm_now
            step_len = norm_next / (product - ratio * norm_next / step_len)
            direction = residual + ratio[:, None, None] * direction
            along = applied + ratio[:, None, None] * along
            norm_now = norm_next
    return (solution, residual)


def solution(mesh):
    placed = (
        P("comp", "dom", None, None, None),
        P("comp", "dom", None),
        P("comp", "dom", None, None),
        P("comp", "dom", None, None, None),
        P("dom", "comp"),
    )
    return jax.shard_map(
        per_device,
        mesh=mesh,
        in_specs=placed,
        out_specs=(P(None, "dom", "comp"), P(None, "dom", "comp")),
        check_vma=False,
    )
```

profile of v0, /device:TPU:0, one launch (start us, length us, event | category | flops | bytes accessed | tf_op | source)
XLA Modules:
  0.0 140.9 jit_solution(12832660203048157975)
XLA Ops:
  0.6 0.0 copy-start
  0.6 0.8 convert_bitcast_fusion
  1.4 0.0 copy-start.2
  1.4 0.2 convert_reduce_fusion
  1.6 0.5 copy-done.2
  2.1 0.1 select_reduce_fusion
  2.2 0.7 sub.21
  2.9 0.0 copy-start.3
  2.9 4.4 %all-to-all-start.1 = ((f32[4,4,1]{1,2,0:T(1,128)}), f32[4,4,1]{1,2,0:T(1,128)S(1)}, u32[]{:S(2)}, u32[]{:S(2)}) async-start(f32[4,4,1]{1,2,0:T(1,128)} %bitcast.8), calls=%async_computation.1 | async-start | bytes 4096 | tf_op jit(solution)/shard_map/all_to_all | solution.py:65
  7.2 0.0 copy-done.3
  7.3 1.5 %gather_fusion = bf16[12,16,128]{2,1,0:T(8,128)(2,1)S(1)} fusion(bf16[32,16,128]{2,1,0:T(8,128)(2,1)} %bitcast.25, s32[1024]{0:T(1024)S(1)} %pad_clamp_fusion), kind=kCustom, calls=%fused_computation | custom fusion | bytes 98352 | tf_op jit(solution)/shard_map/jit(_take)/gather | solution.py:46
  8.8 0.0 copy-done
  8.8 0.3 fusion
  9.1 0.3 fusion.11
  9.5 0.7 copy.11
  10.2 0.8 all-to-all-done.1
  11.0 3.3 %all-to-all-start = ((f32[16,16,128]{2,1,0:T(8,128)}), f32[16,16,128]{2,1,0:T(8,128)S(1)}, u32[]{:S(2)}, u32[]{:S(2)}) async-start(f32[16,16,128]{2,1,0:T(8,128)} %copy.11), calls=%async_computation | async-start | bytes 262144 | tf_op jit(solution)/shard_map/all_to_all | solution.py:64
  14.3 0.1 convert_element_type.29
  14.4 4.5 %all-to-all-done = f32[16,16,128]{2,1,0:T(8,128)S(1)} async-done(((f32[16,16,128]{2,1,0:T(8,128)}), f32[16,16,128]{2,1,0:T(8,128)S(1)}, u32[]{:S(2)}, u32[]{:S(2)}) %all-to-all-start) | async-done | bytes 131104 | tf_op jit(solution)/shard_map/all_to_all | solution.py:64
  18.9 0.4 convolution_bitcast_fusion
  19.2 0.1 fusion.27
  19.4 1.3 collective-permute-start.1
  20.7 0.0 copy-start.1
  20.7 3.0 %collective-permute-start = (f32[16,32,1]{2,1,0:T(8,128)S(1)}, f32[16,32,1]{2,1,0:T(8,128)S(1)}, u32[]{:S(2)}, u32[]{:S(2)}) collective-permute-start(f32[16,32,1]{2,1,0:T(8,128)S(1)} %get-tuple-element.22), channel_id=1, source_target_pairs={{0,8},{8,16},{16,24},{1,9},{9,17},{17,25},{2,10},{10,18},{18,26},{... | collective-permute-start | bytes 6152 | tf_op jit(solution)/shard_map/ppermute | solution.py:20
  23.8 0.0 collective-permute-done.1
  23.8 1.1 collective-permute-done
  24.9 0.2 pad_maximum_fusion.21
  25.1 1.3 collective-permute-start.2
  26.4 4.5 %collective-permute-start.3 = (f32[16,1,130]{2,1,0:T(1,128)S(1)}, f32[16,1,130]{2,1,0:T(1,128)S(1)}, u32[]{:S(2)}, u32[]{:S(2)}) collective-permute-start(f32[16,1,130]{2,1,0:T(1,128)S(1)} %get-tuple-element.16), channel_id=1, source_target_pairs={{0,1},{1,2},{2,3},{3,4},{4,5},{5,6},{6,7},{8,9},{9,10},{10,11},{11... | collective-permute-start | bytes 24968 | tf_op jit(solution)/shard_map/ppermute | solution.py:20
  30.9 0.0 copy-done.1
  30.9 0.0 collective-permute-done.2
  30.9 1.4 collective-permute-done.3
  32.3 0.8 multiply_reduce_fusion.2
  33.1 45.7 %all-reduce.1 = (f32[16]{0:T(128)S(1)}, f32[16]{0:T(128)S(1)}) all-reduce(f32[16]{0:T(128)S(1)} %get-tuple-element.5, f32[16]{0:T(128)S(1)} %get-tuple-element.4), channel_id=1, replica_groups=mesh['comp'=4,'dom'=8] {'comp','dom'}, use_global_device_ids=true, to_apply=%region_3.4 | all-reduce | flops 32 | bytes 256 | tf_op jit(solution)/shard_map/psum | solution.py:37
  78.8 0.1 multiply_subtract_fusion.1
  78.9 0.1 fusion.26
  79.1 1.3 collective-permute-start.5
  80.4 3.0 %collective-permute-start.4 = (f32[16,32,1]{2,1,0:T(8,128)S(1)}, f32[16,32,1]{2,1,0:T(8,128)S(1)}, u32[]{:S(2)}, u32[]{:S(2)}) collective-permute-start(f32[16,32,1]{2,1,0:T(8,128)S(1)} %get-tuple-element.20), channel_id=1, source_target_pairs={{0,8},{8,16},{16,24},{1,9},{9,17},{17,25},{2,10},{10,18},{18,26},{... | collective-permute-start | bytes 6152 | tf_op jit(solution)/shard_map/ppermute | solution.py:20
  83.4 0.0 collective-permute-done.5
  83.4 1.1 collective-permute-done.4
  84.5 0.2 pad_maximum_fusion.18
  84.7 1.3 collective-permute-start.6
  86.0 4.8 %collective-permute-start.7 = (f32[16,1,130]{2,1,0:T(1,128)S(1)}, f32[16,1,130]{2,1,0:T(1,128)S(1)}, u32[]{:S(2)}, u32[]{:S(2)}) collective-permute-start(f32[16,1,130]{2,1,0:T(1,128)S(1)} %get-tuple-element.14), channel_id=1, source_target_pairs={{0,1},{1,2},{2,3},{3,4},{4,5},{5,6},{6,7},{8,9},{9,10},{10,11},{11... | collective-permute-start | bytes 24968 | tf_op jit(solution)/shard_map/ppermute | solution.py:20
  90.8 0.0 collective-permute-done.6
  90.8 1.4 %collective-permute-done.7 = f32[16,1,130]{2,1,0:T(1,128)S(1)} collective-permute-done((f32[16,1,130]{2,1,0:T(1,128)S(1)}, f32[16,1,130]{2,1,0:T(1,128)S(1)}, u32[]{:S(2)}, u32[]{:S(2)}) %collective-permute-start.7) | collective-permute-done | bytes 8352 | tf_op jit(solution)/shard_map/ppermute | solution.py:20
  92.3 0.8 multiply_reduce_fusion
  93.0 46.6 %all-reduce = (f32[16]{0:T(128)S(1)}, f32[16]{0:T(128)S(1)}) all-reduce(f32[16]{0:T(128)S(1)} %get-tuple-element.3, f32[16]{0:T(128)S(1)} %get-tuple-element.2), channel_id=1, replica_groups=mesh['comp'=4,'dom'=8] {'comp','dom'}, use_global_device_ids=true, to_apply=%region_7.8 | all-reduce | flops 32 | bytes 256 | tf_op jit(solution)/shard_map/psum | solution.py:37
  139.6 1.2 multiply_subtract_fusion
  (9 shorter events, 0.1 us)
Async XLA Ops:
  0.6 8.1 %copy-start = (bf16[1,1,12,128,128]{4,3,2,1,0:T(8,128)(2,1)S(1)}, bf16[1,1,12,128,128]{4,3,2,1,0:T(8,128)(2,1)}, u32[]{:S(2)}) copy-start(bf16[1,1,12,128,128]{4,3,2,1,0:T(8,128)(2,1)} %param.8) | copy-start | bytes 1179652
  1.4 0.7 copy-start.2
  2.9 4.4 %copy-start.3 = (s32[1,1,12]{2,1,0:T(1,128)S(1)}, s32[1,1,12]{2,1,0:T(1,128)}, u32[]{:S(2)}) copy-start(s32[1,1,12]{2,1,0:T(1,128)} %param.6) | copy-start | bytes 148
  2.9 8.1 %all-to-all-start.1 = ((f32[4,4,1]{1,2,0:T(1,128)}), f32[4,4,1]{1,2,0:T(1,128)S(1)}, u32[]{:S(2)}, u32[]{:S(2)}) async-start(f32[4,4,1]{1,2,0:T(1,128)} %bitcast.8), calls=%async_computation.1 | async-start | bytes 4096 | tf_op jit(solution)/shard_map/all_to_all | solution.py:65
  11.0 7.9 %all-to-all-start = ((f32[16,16,128]{2,1,0:T(8,128)}), f32[16,16,128]{2,1,0:T(8,128)S(1)}, u32[]{:S(2)}, u32[]{:S(2)}) async-start(f32[16,16,128]{2,1,0:T(8,128)} %copy.11), calls=%async_computation | async-start | bytes 262144 | tf_op jit(solution)/shard_map/all_to_all | solution.py:64
  19.4 4.4 %collective-permute-start.1 = (f32[16,32,1]{2,1,0:T(8,128)S(1)}, f32[16,32,1]{2,1,0:T(8,128)S(1)}, u32[]{:S(2)}, u32[]{:S(2)}) collective-permute-start(f32[16,32,1]{2,1,0:T(8,128)S(1)} %get-tuple-element.21), channel_id=1, source_target_pairs={{8,0},{16,8},{24,16},{9,1},{17,9},{25,17},{10,2},{18,10},{26,18},{... | collective-permute-start | bytes 6152 | tf_op jit(solution)/shard_map/ppermute | solution.py:21
  20.7 10.2 %copy-start.1 = (f32[32,128]{1,0:T(8,128)S(1)}, f32[32,128]{1,0:T(8,128)}, u32[]{:S(2)}) copy-start(f32[32,128]{1,0:T(8,128)} %param.9) | copy-start | bytes 49156
  20.7 4.2 %collective-permute-start = (f32[16,32,1]{2,1,0:T(8,128)S(1)}, f32[16,32,1]{2,1,0:T(8,128)S(1)}, u32[]{:S(2)}, u32[]{:S(2)}) collective-permute-start(f32[16,32,1]{2,1,0:T(8,128)S(1)} %get-tuple-element.22), channel_id=1, source_target_pairs={{0,8},{8,16},{16,24},{1,9},{9,17},{17,25},{2,10},{10,18},{18,26},{... | collective-permute-start | bytes 6152 | tf_op jit(solution)/shard_map/ppermute | solution.py:20
  25.1 5.9 %collective-permute-start.2 = (f32[16,1,130]{2,1,0:T(1,128)S(1)}, f32[16,1,130]{2,1,0:T(1,128)S(1)}, u32[]{:S(2)}, u32[]{:S(2)}) collective-permute-start(f32[16,1,130]{2,1,0:T(1,128)S(1)} %get-tuple-element.15), channel_id=1, source_target_pairs={{1,0},{2,1},{3,2},{4,3},{5,4},{6,5},{7,6},{9,8},{10,9},{11,10},{12... | collective-permute-start | bytes 24968 | tf_op jit(solution)/shard_map/ppermute | solution.py:21
  26.4 6.0 %collective-permute-start.3 = (f32[16,1,130]{2,1,0:T(1,128)S(1)}, f32[16,1,130]{2,1,0:T(1,128)S(1)}, u32[]{:S(2)}, u32[]{:S(2)}) collective-permute-start(f32[16,1,130]{2,1,0:T(1,128)S(1)} %get-tuple-element.16), channel_id=1, source_target_pairs={{0,1},{1,2},{2,3},{3,4},{4,5},{5,6},{6,7},{8,9},{9,10},{10,11},{11... | collective-permute-start | bytes 24968 | tf_op jit(solution)/shard_map/ppermute | solution.py:20
  79.1 4.4 %collective-permute-start.5 = (f32[16,32,1]{2,1,0:T(8,128)S(1)}, f32[16,32,1]{2,1,0:T(8,128)S(1)}, u32[]{:S(2)}, u32[]{:S(2)}) collective-permute-start(f32[16,32,1]{2,1,0:T(8,128)S(1)} %get-tuple-element.19), channel_id=1, source_target_pairs={{8,0},{16,8},{24,16},{9,1},{17,9},{25,17},{10,2},{18,10},{26,18},{... | collective-permute-start | bytes 6152 | tf_op jit(solution)/shard_map/ppermute | solution.py:21
  80.4 4.2 %collective-permute-start.4 = (f32[16,32,1]{2,1,0:T(8,128)S(1)}, f32[16,32,1]{2,1,0:T(8,128)S(1)}, u32[]{:S(2)}, u32[]{:S(2)}) collective-permute-start(f32[16,32,1]{2,1,0:T(8,128)S(1)} %get-tuple-element.20), channel_id=1, source_target_pairs={{0,8},{8,16},{16,24},{1,9},{9,17},{17,25},{2,10},{10,18},{18,26},{... | collective-permute-start | bytes 6152 | tf_op jit(solution)/shard_map/ppermute | solution.py:20
  84.7 6.1 %collective-permute-start.6 = (f32[16,1,130]{2,1,0:T(1,128)S(1)}, f32[16,1,130]{2,1,0:T(1,128)S(1)}, u32[]{:S(2)}, u32[]{:S(2)}) collective-permute-start(f32[16,1,130]{2,1,0:T(1,128)S(1)} %get-tuple-element.13), channel_id=1, source_target_pairs={{1,0},{2,1},{3,2},{4,3},{5,4},{6,5},{7,6},{9,8},{10,9},{11,10},{12... | collective-permute-start | bytes 24968 | tf_op jit(solution)/shard_map/ppermute | solution.py:21
  86.0 6.2 %collective-permute-start.7 = (f32[16,1,130]{2,1,0:T(1,128)S(1)}, f32[16,1,130]{2,1,0:T(1,128)S(1)}, u32[]{:S(2)}, u32[]{:S(2)}) collective-permute-start(f32[16,1,130]{2,1,0:T(1,128)S(1)} %get-tuple-element.14), channel_id=1, source_target_pairs={{0,1},{1,2},{2,3},{3,4},{4,5},{5,6},{6,7},{8,9},{9,10},{10,11},{11... | collective-permute-start | bytes 24968 | tf_op jit(solution)/shard_map/ppermute | solution.py:20
where the time goes:
time: 141 us
  blocking collectives  92.3 us (65%)
  starting transfers between devices  28.3 us (20%)
  waiting for transfers between devices  10.3 us (7%)
  other arithmetic  4.26 us (3%)
  local copies, waits for them, and re-layouts  3.7 us (3%)
    psum x2, blocking collectives, two_products(): lax.psum((row_dots(residual, residual), row_dots(residual, applied)), ('c...  92.3 us
    ppermute x4, starting transfers between devices, with_halo(): before = lax.ppermute(last, axis, up)  15.4 us
    ppermute x4, starting transfers between devices, with_halo(): after = lax.ppermute(initial, axis, down)  5.17 us
    ppermute x4, waiting for transfers between devices, with_halo(): before = lax.ppermute(last, axis, up)  5.04 us
    all_to_all x1, waiting for transfers between devices, per_device(): lax.all_to_all(outgoing, 'comp', split_axis=0, concat_axis=0, tiled=True)  4.46 us
    all_to_all x1, starting transfers between devices, per_device(): lax.all_to_all(labels, 'comp', split_axis=0, concat_axis=0, tiled=True)  4.4 us
    all_to_all x1, starting transfers between devices, per_device(): lax.all_to_all(outgoing, 'comp', split_axis=0, concat_axis=0, tiled=True)  3.33 us
  transfers between devices with their start and end apart: 10, of which 6 were waited for; matrix products, arithmetic and copies ran while one was open for 2% of the time, Pallas kernels for 0%

commit v1 on v0

v1 whole, which is shorter than its diff:
```python
import functools
import jax
import jax.numpy as jnp
from jax import lax
from jax.experimental import pallas as pl
from jax.experimental.pallas import tpu as pltpu
from jax.sharding import PartitionSpec as P

HALF = 2
LANES = 128
LABEL = 8
HELM = 16
SHIFT = 4.0

VMEM = pl.BlockSpec(memory_space=pltpu.VMEM)
SMEM = pl.BlockSpec(memory_space=pltpu.SMEM)


def call(kernel, out_shape, in_specs, scratch=(), name=None):
    return pl.pallas_call(
        kernel,
        out_shape=out_shape,
        in_specs=in_specs,
        out_specs=jax.tree.map(lambda _: VMEM, out_shape),
        scratch_shapes=scratch,
        name=name,
        compiler_params=pltpu.CompilerParams(vmem_limit_bytes=16 * 1024 * 1024),
    )


def peer_of(me, step, devices):
    if devices & (devices - 1) == 0:
        return me ^ step, me ^ step
    return lax.rem(me + step, devices), lax.rem(me + devices - step, devices)


def lane_ids(rows):
    return lax.broadcasted_iota(jnp.int32, (rows, LANES), 1)


def pack_kernel(groups, ids, margin, sources, weights, helm, *rest):
    messages, (slots, labels) = rest[:groups], rest[groups:]
    levels = sources.shape[1]
    entries = ids.shape[0]
    slots[...] = jnp.zeros_like(slots)
    for at in range((groups + 2) * HALF):
        labels[at] = -1
    for k in range(entries):
        base = (margin[0, k] + 1) * HALF
        row = margin[1, k]
        first = labels[base]
        later = jnp.logical_and(first >= 0, first != row).astype(jnp.int32)
        labels[base + later] = row
        part = lax.dot_general(
            sources[ids[k]], weights[k], (((1,), (1,)), ((), ())), preferred_element_type=jnp.float32
        )
        slots[base + later] += part
    me = lax.axis_index("comp")
    lane = lane_ids(levels)
    lane8 = lane_ids(8)
    packed = jnp.zeros((8, LANES), jnp.float32)
    for g in range(helm.shape[0] // 8):
        at = HELM + 2 * g
        turned = pltpu.roll(helm[8 * g : 8 * g + 8, :], at + 1, 1)
        packed = jnp.where((lane8 == at) | (lane8 == at + 1), turned, packed)
    packed = jnp.concatenate([packed, jnp.zeros((levels - 8, LANES), jnp.float32)], axis=0)
    for step in range(groups):
        to, _ = peer_of(me, step, groups)
        base = (to + 1) * HALF
        out = messages[step]
        out[0] = slots[base]
        out[1] = slots[base + 1]
        left, right = base - HALF, base + HALF
        side = jnp.where(lane < 2, slots[right], packed)
        side = jnp.where(lane >= LANES - 2, slots[left], side)
        side = jnp.where((lane >= 2) & (lane < 4), pltpu.roll(slots[right + 1], 2, 1), side)
        side = jnp.where(
            (lane >= LANES - 4) & (lane < LANES - 2), pltpu.roll(slots[left + 1], LANES - 2, 1), side
        )
        for j, at in enumerate((base, base + 1, left, left + 1, right, right + 1)):
            side = jnp.where(lane == LABEL + j, labels[at].astype(jnp.float32), side)
        out[2] = side


def assemble_kernel(groups, helm, *rest):
    messages, (field, outer, helm_outer, swap_a, swap_b) = rest[:groups], rest[groups:]
    rows, levels, _ = field.shape
    me = lax.axis_index("comp")
    lane = lane_ids(levels)
    lane8 = lane_ids(8)
    blocks, tags, cols, col_tags = [], [], [], []
    for g in range(rows // 8):
        helm_outer[8 * g : 8 * g + 8, :] = jnp.zeros((8, LANES), jnp.float32)
    for step in range(groups):
        _, source = peer_of(me, step, groups)
        got = messages[step]
        side = got[2]

        def tag(j):
            return jnp.broadcast_to(side[:, LABEL + j : LABEL + j + 1], side.shape)

        blocks += [got[0], got[1]]
        tags += [tag(0), tag(1)]
        cols.append(jnp.where((lane < 2) | (lane >= LANES - 2), side, 0.0))
        col_tags.append(jnp.where(lane < LANES // 2, tag(4), tag(2)))
        inner = jnp.where(lane < LANES // 2, pltpu.roll(side, LANES - 2, 1), pltpu.roll(side, 2, 1))
        cols.append(jnp.where((lane < 2) | (lane >= LANES - 2), inner, 0.0))
        col_tags.append(jnp.where(lane < LANES // 2, tag(5), tag(3)))
        if step:
            top = side[:8]
            for g in range(rows // 8):
                turned = pltpu.roll(top, LANES - (HELM + 2 * g + 1), 1)
                mine = ((lane8 == LANES - 1) & (source == me - 1)) | ((lane8 == 0) & (source == me + 1))
                at = pl.ds(8 * g, 8)
                helm_outer[at, :] = jnp.where(mine, turned, helm_outer[at, :])

    def total(parts):
        while len(parts) > 1:
            parts = [a + b for a, b in zip(parts[::2], parts[1::2])] + parts[len(parts) // 2 * 2 :]
        return parts[0]

    for row in range(rows):
        at = float(row)
        field[row] = total([jnp.where(t == at, b, 0.0) for t, b in zip(tags, blocks)])
        outer[row] = total([jnp.where(t == at, b, 0.0) for t, b in zip(col_tags, cols)])
    even = lax.rem(lax.axis_index("dom"), 2) == 0
    for out, low in ((swap_a, jnp.logical_not(even)), (swap_b, even)):
        edge = jnp.where(low, 0, rows - 1)
        beyond = jnp.where(low, 1, rows - 2)
        out[0:levels] = field[edge]
        out[levels : 2 * levels] = field[beyond]
        out[2 * levels : 3 * levels] = outer[edge]
        out[3 * levels :] = jnp.broadcast_to(helm[pl.ds(edge, 1), :], (8, LANES))


def moments_kernel(helm, helm_outer, field, outer, got_a, got_b, image, second, partial):
    rows, levels, _ = field.shape
    comp, comps = lax.axis_index("comp"), lax.axis_size("comp")
    dom, doms = lax.axis_index("dom"), lax.axis_size("dom")
    even = lax.rem(dom, 2) == 0
    lane = lane_ids(levels)
    first, last = lane == 0, lane == LANES - 1

    def left(x, beside):
        return pltpu.roll(jnp.where(last, beside, x), 1, 1)

    def right(x, beside):
        return pltpu.roll(jnp.where(first, beside, x), LANES - 1, 1)

    def halo(at):
        a, b = got_a[at], got_b[at]
        return jnp.where(even, b, a), jnp.where(even, a, b)

    near, far = pl.ds(0, levels), pl.ds(levels, levels)
    corner, coef = pl.ds(2 * levels, levels), pl.ds(3 * levels, 1)
    above, below = halo(near)
    above2, below2 = halo(far)
    above_outer, below_outer = halo(corner)
    helm_above, helm_below = halo(coef)

    def r(i):
        return above2 if i == -2 else above if i == -1 else below if i == rows else below2 if i == rows + 1 else field[i]

    def e(i):
        return above_outer if i == -1 else below_outer if i == rows else outer[i]

    def h(i):
        return helm_above if i == -1 else helm_below if i == rows else helm[i : i + 1, :]

    def apply(i):
        x = r(i)
        return h(i) * x - ((left(x, e(i)) + right(x, e(i))) + (r(i - 1) + r(i + 1)))

    inside = (last & (comp > 0)) | (first & (comp < comps - 1))
    before = jnp.where(dom > 0, apply(-1), 0.0)
    after = jnp.where(dom < doms - 1, apply(rows), 0.0)
    for i in range(rows):
        image[i] = apply(i)
    sums = [jnp.zeros((levels, LANES), jnp.float32) for _ in range(4)]
    for i in range(rows):
        x, beside, u = field[i], outer[i], image[i]
        out = helm_outer[i : i + 1, :] * beside - ((left(beside, x) + right(beside, x)) + (e(i - 1) + e(i + 1)))
        out = jnp.where(inside, out, 0.0)
        up = before if i == 0 else image[i - 1]
        down = after if i == rows - 1 else image[i + 1]
        z = helm[i : i + 1, :] * u - ((left(u, out) + right(u, out)) + (up + down))
        second[i] = z
        for j, (a, b) in enumerate(((x, x), (x, u), (u, u), (u, z))):
            sums[j] = sums[j] + a * b
    stacked = jnp.concatenate(sums + [jnp.zeros((LANES - 4 * levels, LANES), jnp.float32)], axis=0)
    line = jnp.sum(stacked.T, axis=0, keepdims=True)
    for d in range(partial.shape[0]):
        partial[d] = line


def final_kernel(partials, field, image, second, solution, residual):
    rows, levels, _ = field.shape
    line = partials[0]
    for d in range(1, partials.shape[0]):
        line = line + partials[d]
    lane = lane_ids(levels)
    level = lax.broadcasted_iota(jnp.int32, (levels, LANES), 0)
    rr, p, q, s = [
        jnp.sum(jnp.where(lane == level + j * levels, line, 0.0), axis=1, keepdims=True) for j in range(4)
    ]
    mean = p / rr
    square = q / rr
    spread = square - mean * mean
    third = s / rr - mean * (3.0 * square - 2.0 * mean * mean)
    along = SHIFT + mean
    a0 = 1.0 / along
    beta = a0 * a0 * spread
    a1 = 1.0 / (third / spread + along - a0 * spread)
    c1 = 1.0 + beta - SHIFT * a0
    wide = lambda x: jnp.broadcast_to(x, (levels, LANES))
    sol_r, sol_u = wide(a0 + a1 * c1), wide(-a1 * a0)
    res_r = wide(1.0 - SHIFT * a0 - SHIFT * a1 * c1)
    res_u = wide(-a0 - a1 * (c1 - SHIFT * a0))
    res_y = wide(a1 * a0)
    for i in range(rows):
        x, u, y = field[i], image[i], second[i]
        at = pl.ds(i, levels, stride=rows)
        solution[at, :] = sol_r * x + sol_u * u
        residual[at, :] = (res_r * x + res_u * u) + res_y * y


def per_device(source_field, source_block, margin, remap_weight, helm):
    sources, weights = source_field[0, 0], remap_weight[0, 0]
    ids, marks = source_block[0, 0], margin[0, 0].T
    groups, doms = lax.axis_size("comp"), lax.axis_size("dom")
    levels = sources.shape[1]
    rows = helm.shape[0]
    f32 = lambda *shape: jax.ShapeDtypeStruct(shape, jnp.float32)
    messages = call(
        functools.partial(pack_kernel, groups),
        [f32(3, levels, LANES)] * groups,
        [SMEM, SMEM, VMEM, VMEM, VMEM],
        [pltpu.VMEM(((groups + 2) * HALF, levels, LANES), jnp.float32), pltpu.SMEM(((groups + 2) * HALF,), jnp.int32)],
        name="pack",
    )(ids, marks, sources, weights, helm)
    arrived = [messages[0]]
    for step in range(1, groups):
        pairs = [(c, int(peer_of(c, step, groups)[0]) if groups & (groups - 1) == 0 else (c + step) % groups) for c in range(groups)]
        arrived.append(lax.ppermute(messages[step], "comp", pairs))
    cube = f32(rows, levels, LANES)
    swap = f32(3 * levels + 8, LANES)
    field, outer, helm_outer, swap_a, swap_b = call(
        functools.partial(assemble_kernel, groups),
        [cube, cube, f32(rows, LANES), swap, swap],
        [VMEM] * (1 + groups),
        name="assemble",
    )(helm, *arrived)
    pairs_a = [(d, d ^ 1) for d in range(doms) if d ^ 1 < doms]
    pairs_b = [(d, e) for d in range(doms) for e in [((d + 1) ^ 1) - 1] if 0 <= e < doms]
    got_b = lax.ppermute(swap_b, "dom", pairs_b)
    got_a = lax.ppermute(swap_a, "dom", pairs_a)
    devices = groups * doms
    image, second, partial = call(
        moments_kernel, [cube, cube, f32(devices, 1, LANES)], [VMEM] * 6, name="moments"
    )(helm, helm_outer, field, outer, got_a, got_b)
    partials = lax.all_to_all(partial, ("comp", "dom"), split_axis=0, concat_axis=0, tiled=True)
    flat = f32(levels * rows, LANES)
    outs = call(final_kernel, [flat, flat], [VMEM] * 4, name="final")(partials, field, image, second)
    return tuple(out.reshape(levels, rows, LANES) for out in outs)


def solution(mesh):
    placed = (
        P("comp", "dom", None, None, None),
        P("comp", "dom", None),
        P("comp", "dom", None, None),
        P("comp", "dom", None, None, None),
        P("dom", "comp"),
    )
    return jax.shard_map(
        per_device,
        mesh=mesh,
        in_specs=placed,
        out_specs=(P(None, "dom", "comp"), P(None, "dom", "comp")),
        check_vma=False,
    )
```

time: 141 us -> 34.7 us (0.25)
  blocking collectives: 92.3 us -> 15.4 us
  starting transfers between devices: 28.3 us -> 5.38 us
  waiting for transfers between devices: 10.3 us -> 4.94 us
  Pallas kernels: 0 us -> 4.75 us
  other arithmetic: 4.26 us -> 0 us
    psum x2 -> x0, blocking collectives: 92.3 us -> none  [two_products(): lax.psum((row_dots(residual, residual), row_dots(residual, applied)), ('c...]
    all_to_all x0 -> x1, blocking collectives: none -> 15.4 us  [per_device(): lax.all_to_all(partial, ('comp', 'dom'), split_axis=0, concat_axis=0, til...]
    ppermute x8 -> x5, starting transfers between devices: 20.6 us -> 5.38 us  [the longest x3 3.18 us: per_device(): arrived.append(lax.ppermute(messages[step], 'comp', pairs))]
    all_to_all x2 -> x0, starting transfers between devices: 7.72 us -> none  [the longest x1 4.4 us: per_device(): lax.all_to_all(labels, 'comp', split_axis=0, concat_axis=0, tiled=True)]
    all_to_all x2 -> x0, waiting for transfers between devices: 5.25 us -> none  [the longest x1 4.46 us: per_device(): lax.all_to_all(outgoing, 'comp', split_axis=0, concat_axis=0, tiled=True)]
    pallas_call x0 -> x4, Pallas kernels: none -> 4.75 us  [the longest x1 1.86 us: per_device(): call(moments_kernel, [cube, cube, f32(devices, 1, LANES)], [VMEM] * 6, na...]
    unnamed x8 -> x12, local copies, waits for them, and re-layouts: 0.52 us -> 3.29 us
    reduce_sum x3 -> x0, other arithmetic: 1.7 us -> none  [the longest x2 1.51 us: row_dots(): return jnp.sum(left * right, axis=(1, 2))]
  transfers between devices with their start and end apart: 10 -> 5, of which waited for: 6 -> 3; matrix products, arithmetic and copies ran while one was open for 2% -> 0% of each run, Pallas kernels for 0% -> 0%
where the time goes in v1:
time: 34.7 us; the launch traced here: 34.4 us
  blocking collectives  15.4 us (44%)
  starting transfers between devices  5.38 us (16%)
  waiting for transfers between devices  4.94 us (14%)
  Pallas kernels  4.75 us (14%)
  local copies, waits for them, and re-layouts  3.29 us (9%)
  between operations  0.68 us (2%)
    all_to_all x1, blocking collectives, per_device(): lax.all_to_all(partial, ('comp', 'dom'), split_axis=0, concat_axis=0, til...  15.4 us
    unnamed x12, local copies, waits for them, and re-layouts  3.29 us
    ppermute x3, waiting for transfers between devices, per_device(): arrived.append(lax.ppermute(messages[step], 'comp', pairs))  3.21 us
    ppermute x3, starting transfers between devices, per_device(): arrived.append(lax.ppermute(messages[step], 'comp', pairs))  3.18 us
    pallas_call x1, Pallas kernels, per_device(): call(moments_kernel, [cube, cube, f32(devices, 1, LANES)], [VMEM] * 6, na...  1.86 us
    ppermute x1, waiting for transfers between devices, per_device(): got_a = lax.ppermute(swap_a, 'dom', pairs_a)  1.72 us
    ppermute x1, starting transfers between devices, per_device(): got_a = lax.ppermute(swap_a, 'dom', pairs_a)  1.55 us
    pallas_call x1, Pallas kernels, per_device(): call(final_kernel, [flat, flat], [VMEM] * 4, name='final')  1.43 us
  transfers between devices with their start and end apart: 5, of which 3 were waited for; matrix products, arithmetic and copies ran while one was open for 0% of the time, Pallas kernels for 0%

profile of v1, /device:TPU:0, one launch (start us, length us, event | category | flops | bytes accessed | tf_op | source)
XLA Modules:
  0.0 34.4 jit_solution(4995400822803407305)
XLA Ops:
  0.6 0.0 copy-start.4
  0.6 0.0 copy-start.5
  0.7 0.7 %copy-done.4 = s32[1,1,12,2]{2,3,1,0:T(2,128)S(1)} copy-done((s32[1,1,12,2]{2,3,1,0:T(2,128)S(1)}, s32[1,1,12,2]{2,3,1,0:T(2,128)}, u32[]{:S(2)}) %copy-start.4) | copy-done | bytes 120
  1.3 0.0 copy-done.5
  1.3 0.0 copy-start
  1.3 1.0 %copy-done = bf16[1,1,12,128,128]{4,3,2,1,0:T(8,128)(2,1)S(1)} copy-done((bf16[1,1,12,128,128]{4,3,2,1,0:T(8,128)(2,1)S(1)}, bf16[1,1,12,128,128]{4,3,2,1,0:T(8,128)(2,1)}, u32[]{:S(2)}) %copy-start) | copy-done | bytes 393240
  2.3 0.0 copy-start.1
  2.3 0.7 %copy-done.1 = f32[32,128]{1,0:T(8,128)S(1)} copy-done((f32[32,128]{1,0:T(8,128)S(1)}, f32[32,128]{1,0:T(8,128)}, u32[]{:S(2)}) %copy-start.1) | copy-done | bytes 16408
  3.0 0.0 copy-start.3
  3.0 0.9 %copy-done.3 = bf16[1,1,32,16,128]{4,3,2,1,0:T(8,128)(2,1)S(1)} copy-done((bf16[1,1,32,16,128]{4,3,2,1,0:T(8,128)(2,1)S(1)}, bf16[1,1,32,16,128]{4,3,2,1,0:T(8,128)(2,1)}, u32[]{:S(2)}) %copy-start.3) | copy-done | bytes 131096
  3.9 0.0 copy-start.2
  3.9 1.0 %pack.1 = (f32[3,16,128]{2,1,0:T(8,128)S(1)}, f32[3,16,128]{2,1,0:T(8,128)S(1)}, f32[3,16,128]{2,1,0:T(8,128)S(1)}, f32[3,16,128]{2,1,0:T(8,128)S(1)}) custom-call(s32[12]{0:T(128)S(1)} %bitcast.11, s32[2,12]{1,0:T(2,128)S(1)} %bitcast.10, bf16[32,16,128]{2,1,0:T(8,128)(2,1)S(1)} %bitcast.9, bf16[12,128,128]{2,1,0:T(8,128)(2,1)S(1)} %bitcast.8, ...), custom_call_target="tpu_custom_call" | custom-call | tf_op jit(solution)/shard_map/pack/pallas_call | solution.py:234
  4.9 0.6 %collective-permute-start = (f32[3,16,128]{2,1,0:T(8,128)S(1)}, f32[3,16,128]{2,1,0:T(8,128)S(1)}, u32[]{:S(2)}, u32[]{:S(2)}) collective-permute-start(f32[3,16,128]{2,1,0:T(8,128)S(1)} %get-tuple-element.17), channel_id=1, source_target_pairs={{0,8},{8,0},{16,24},{24,16},{1,9},{9,1},{17,25},{25,17},{2,10},{10... | collective-permute-start | bytes 73736 | tf_op jit(solution)/shard_map/ppermute | solution.py:244
  5.5 2.6 %collective-permute-start.1 = (f32[3,16,128]{2,1,0:T(8,128)S(1)}, f32[3,16,128]{2,1,0:T(8,128)S(1)}, u32[]{:S(2)}, u32[]{:S(2)}) collective-permute-start(f32[3,16,128]{2,1,0:T(8,128)S(1)} %get-tuple-element.18), channel_id=1, source_target_pairs={{0,16},{8,24},{16,0},{24,8},{1,17},{9,25},{17,1},{25,9},{2,18},{10... | collective-permute-start | bytes 73736 | tf_op jit(solution)/shard_map/ppermute | solution.py:244
  8.0 0.0 collective-permute-start.2
  8.1 0.0 collective-permute-done.rest_1_
  8.1 1.8 %collective-permute-done.1.rest_2_ = f32[3,16,128]{2,1,0:T(8,128)S(1)} collective-permute-done((f32[3,16,128]{2,1,0:T(8,128)S(1)}, f32[3,16,128]{2,1,0:T(8,128)S(1)}, u32[]{:S(2)}, u32[]{:S(2)}) %collective-permute-start.1) | collective-permute-done | bytes 24608 | tf_op jit(solution)/shard_map/ppermute | solution.py:244
  9.9 1.4 %collective-permute-done.2.rest_3_ = f32[3,16,128]{2,1,0:T(8,128)S(1)} collective-permute-done((f32[3,16,128]{2,1,0:T(8,128)S(1)}, f32[3,16,128]{2,1,0:T(8,128)S(1)}, u32[]{:S(2)}, u32[]{:S(2)}) %collective-permute-start.2) | collective-permute-done | bytes 24608 | tf_op jit(solution)/shard_map/ppermute | solution.py:244
  11.3 0.0 copy-done.2
  11.3 0.5 %assemble.1 = (f32[32,16,128]{2,1,0:T(8,128)S(1)}, f32[32,16,128]{2,1,0:T(8,128)S(1)}, f32[32,128]{1,0:T(8,128)S(1)}, f32[56,128]{1,0:T(8,128)S(1)}, f32[56,128]{1,0:T(8,128)S(1)}) custom-call(f32[32,128]{1,0:T(8,128)S(1)} %copy-done.2, f32[3,16,128]{2,1,0:T(8,128)S(1)} %get-tuple-element.16.rest_0_, f32[3,16,128]{2,1,0:T(8,128)S(1)} %collective-permute-done.rest_1_, ...), custom_call_target="tpu_custom_call" | custom-call | tf_op jit(solution)/shard_map/assemble/pallas_call | solution.py:247
  11.8 1.6 %collective-permute-start.3 = (f32[56,128]{1,0:T(8,128)S(1)}, f32[56,128]{1,0:T(8,128)S(1)}, u32[]{:S(2)}, u32[]{:S(2)}) collective-permute-start(f32[56,128]{1,0:T(8,128)S(1)} %get-tuple-element.23), channel_id=1, source_target_pairs={{0,1},{1,0},{2,3},{3,2},{4,5},{5,4},{6,7},{7,6},{8,9},{9,8},{10,11... | collective-permute-start | bytes 86024 | tf_op jit(solution)/shard_map/ppermute | solution.py:256
  13.3 0.7 %collective-permute-start.4 = (f32[56,128]{1,0:T(8,128)S(1)}, f32[56,128]{1,0:T(8,128)S(1)}, u32[]{:S(2)}, u32[]{:S(2)}) collective-permute-start(f32[56,128]{1,0:T(8,128)S(1)} %get-tuple-element.24), channel_id=1, source_target_pairs={{1,2},{2,1},{3,4},{4,3},{5,6},{6,5},{9,10},{10,9},{11,12},{12,11},... | collective-permute-start | bytes 86024 | tf_op jit(solution)/shard_map/ppermute | solution.py:255
  14.0 1.7 %collective-permute-done.3.got_a = f32[56,128]{1,0:T(8,128)S(1)} collective-permute-done((f32[56,128]{1,0:T(8,128)S(1)}, f32[56,128]{1,0:T(8,128)S(1)}, u32[]{:S(2)}, u32[]{:S(2)}) %collective-permute-start.3) | collective-permute-done | bytes 28704 | tf_op jit(solution)/shard_map/ppermute | solution.py:256
  15.7 0.0 collective-permute-done.4.got_b
  15.7 1.9 %moments.1 = (f32[32,16,128]{2,1,0:T(8,128)S(1)}, f32[32,16,128]{2,1,0:T(8,128)S(1)}, f32[32,1,128]{2,1,0:T(1,128)S(1)}) custom-call(f32[32,128]{1,0:T(8,128)S(1)} %copy-done.2, f32[32,128]{1,0:T(8,128)S(1)} %get-tuple-element.20.helm_outer, f32[32,16,128]{2,1,0:T(8,128)S(1)} %get-tuple-element.21.field, f32[32,16,128]{2,1,0:T(8,128)S(1)} %get-tuple-element.22.outer, ...), custom_call_target="tpu_custom_call" | custom-call | tf_op jit(solution)/shard_map/moments/pallas_call | solution.py:258
  17.6 15.4 %all_to_all.5.partials = f32[32,1,128]{2,1,0:T(1,128)S(1)} all-to-all(f32[32,1,128]{2,1,0:T(1,128)S(1)} %get-tuple-element.25), channel_id=1, replica_groups=mesh['comp'=4,'dom'=8] {'comp','dom'}, dimensions={0} | all-to-all | bytes 32768 | tf_op jit(solution)/shard_map/all_to_all | solution.py:261
  33.0 1.4 %final.1 = (f32[512,128]{1,0:T(8,128)}, f32[512,128]{1,0:T(8,128)}) custom-call(f32[32,1,128]{2,1,0:T(1,128)S(1)} %all_to_all.5.partials, f32[32,16,128]{2,1,0:T(8,128)S(1)} %get-tuple-element.21.field, f32[32,16,128]{2,1,0:T(8,128)S(1)} %get-tuple-element.26.image, f32[32,16,128]{2,1,0:T(8,128)S(1)} %get-tuple-element.27.second), custom_call_target="tpu_custom_call" | custom-call | tf_op jit(solution)/shard_map/final/pallas_call | solution.py:263
Async XLA Ops:
  0.6 0.7 %copy-start.4 = (s32[1,1,12,2]{2,3,1,0:T(2,128)S(1)}, s32[1,1,12,2]{2,3,1,0:T(2,128)}, u32[]{:S(2)}) copy-start(s32[1,1,12,2]{2,3,1,0:T(2,128)} %param.7) | copy-start | bytes 292
  0.6 0.7 %copy-start.5 = (s32[1,1,12]{2,1,0:T(1,128)S(1)}, s32[1,1,12]{2,1,0:T(1,128)}, u32[]{:S(2)}) copy-start(s32[1,1,12]{2,1,0:T(1,128)} %param.6) | copy-start | bytes 148
  1.3 1.0 %copy-start = (bf16[1,1,12,128,128]{4,3,2,1,0:T(8,128)(2,1)S(1)}, bf16[1,1,12,128,128]{4,3,2,1,0:T(8,128)(2,1)}, u32[]{:S(2)}) copy-start(bf16[1,1,12,128,128]{4,3,2,1,0:T(8,128)(2,1)} %param.8) | copy-start | bytes 1179652
  2.3 0.7 %copy-start.1 = (f32[32,128]{1,0:T(8,128)S(1)}, f32[32,128]{1,0:T(8,128)}, u32[]{:S(2)}) copy-start(f32[32,128]{1,0:T(8,128)} %helm.5) | copy-start | bytes 49156
  3.0 0.9 %copy-start.3 = (bf16[1,1,32,16,128]{4,3,2,1,0:T(8,128)(2,1)S(1)}, bf16[1,1,32,16,128]{4,3,2,1,0:T(8,128)(2,1)}, u32[]{:S(2)}) copy-start(bf16[1,1,32,16,128]{4,3,2,1,0:T(8,128)(2,1)} %param.5) | copy-start | bytes 393220
  3.9 7.4 %copy-start.2 = (f32[32,128]{1,0:T(8,128)S(1)}, f32[32,128]{1,0:T(8,128)}, u32[]{:S(2)}) copy-start(f32[32,128]{1,0:T(8,128)} %helm.5) | copy-start | bytes 49156
  4.9 3.2 %collective-permute-start = (f32[3,16,128]{2,1,0:T(8,128)S(1)}, f32[3,16,128]{2,1,0:T(8,128)S(1)}, u32[]{:S(2)}, u32[]{:S(2)}) collective-permute-start(f32[3,16,128]{2,1,0:T(8,128)S(1)} %get-tuple-element.17), channel_id=1, source_target_pairs={{0,8},{8,0},{16,24},{24,16},{1,9},{9,1},{17,25},{25,17},{2,10},{10... | collective-permute-start | bytes 73736 | tf_op jit(solution)/shard_map/ppermute | solution.py:244
  5.5 4.4 %collective-permute-start.1 = (f32[3,16,128]{2,1,0:T(8,128)S(1)}, f32[3,16,128]{2,1,0:T(8,128)S(1)}, u32[]{:S(2)}, u32[]{:S(2)}) collective-permute-start(f32[3,16,128]{2,1,0:T(8,128)S(1)} %get-tuple-element.18), channel_id=1, source_target_pairs={{0,16},{8,24},{16,0},{24,8},{1,17},{9,25},{17,1},{25,9},{2,18},{10... | collective-permute-start | bytes 73736 | tf_op jit(solution)/shard_map/ppermute | solution.py:244
  8.0 3.3 %collective-permute-start.2 = (f32[3,16,128]{2,1,0:T(8,128)S(1)}, f32[3,16,128]{2,1,0:T(8,128)S(1)}, u32[]{:S(2)}, u32[]{:S(2)}) collective-permute-start(f32[3,16,128]{2,1,0:T(8,128)S(1)} %get-tuple-element.19), channel_id=1, source_target_pairs={{0,24},{8,16},{16,8},{24,0},{1,25},{9,17},{17,9},{25,1},{2,26},{10... | collective-permute-start | bytes 73736 | tf_op jit(solution)/shard_map/ppermute | solution.py:244
  11.8 3.9 %collective-permute-start.3 = (f32[56,128]{1,0:T(8,128)S(1)}, f32[56,128]{1,0:T(8,128)S(1)}, u32[]{:S(2)}, u32[]{:S(2)}) collective-permute-start(f32[56,128]{1,0:T(8,128)S(1)} %get-tuple-element.23), channel_id=1, source_target_pairs={{0,1},{1,0},{2,3},{3,2},{4,5},{5,4},{6,7},{7,6},{8,9},{9,8},{10,11... | collective-permute-start | bytes 86024 | tf_op jit(solution)/shard_map/ppermute | solution.py:256
  13.3 2.4 %collective-permute-start.4 = (f32[56,128]{1,0:T(8,128)S(1)}, f32[56,128]{1,0:T(8,128)S(1)}, u32[]{:S(2)}, u32[]{:S(2)}) collective-permute-start(f32[56,128]{1,0:T(8,128)S(1)} %get-tuple-element.24), channel_id=1, source_target_pairs={{1,2},{2,1},{3,4},{4,3},{5,6},{6,5},{9,10},{10,9},{11,12},{12,11},... | collective-permute-start | bytes 86024 | tf_op jit(solution)/shard_map/ppermute | solution.py:255

commit v2 on v1

v2 whole, which is shorter than its diff:
```python
import functools
import jax
import jax.numpy as jnp
from jax import lax
from jax.experimental import pallas as pl
from jax.experimental.pallas import tpu as pltpu
from jax.sharding import PartitionSpec as P

HALF = 2
LANES = 128
LABEL = 8
HELM = 16
SHIFT = 4.0
CHUNKS = 4

VMEM = pl.BlockSpec(memory_space=pltpu.VMEM)
HBM = pl.BlockSpec(memory_space=pltpu.HBM)


def call(kernel, out_shape, in_specs, scratch=(), name=None, out_spec=VMEM, flops=0):
    return pl.pallas_call(
        kernel,
        out_shape=out_shape,
        in_specs=in_specs,
        out_specs=jax.tree.map(lambda _: out_spec, out_shape),
        scratch_shapes=scratch,
        name=name,
        compiler_params=pltpu.CompilerParams(vmem_limit_bytes=16 * 1024 * 1024),
        cost_estimate=pl.CostEstimate(flops=flops, bytes_accessed=flops // 8, transcendentals=0) if flops else None,
    )


def peer_of(me, step, devices):
    if devices & (devices - 1) == 0:
        return me ^ step, me ^ step
    return lax.rem(me + step, devices), lax.rem(me + devices - step, devices)


def lane_ids(rows):
    return lax.broadcasted_iota(jnp.int32, (rows, LANES), 1)


def left(x, beside):
    return pltpu.roll(jnp.where(lane_ids(x.shape[0]) == LANES - 1, beside, x), 1, 1)


def right(x, beside):
    return pltpu.roll(jnp.where(lane_ids(x.shape[0]) == 0, beside, x), LANES - 1, 1)


def across(h, x, beside):
    return h * x - (left(x, beside) + right(x, beside))


def total(parts):
    while len(parts) > 1:
        parts = [a + b for a, b in zip(parts[::2], parts[1::2])] + parts[len(parts) // 2 * 2 :]
    return parts[0]


def pack_kernel(groups, ids_in, margin_in, sources_in, weights_in, helm_in, *rest):
    messages = rest[:groups]
    slots, labels, ids, margin, sources, weights, helm, sems = rest[groups:]
    levels = sources.shape[1]
    entries = ids.shape[0]
    copies = [
        pltpu.make_async_copy(src, dst, sems.at[j])
        for j, (src, dst) in enumerate(((margin_in, margin), (ids_in, ids), (sources_in, sources), (helm_in, helm)))
    ]
    cuts = [entries * j // CHUNKS for j in range(CHUNKS + 1)]
    chunks = []
    for j, (lo, hi) in enumerate(zip(cuts, cuts[1:])):
        at = pl.ds(lo, hi - lo)
        chunks.append(pltpu.make_async_copy(weights_in.at[at], weights.at[at], sems.at[len(copies) + j]))
    for copy in copies[:3] + chunks + copies[3:]:
        copy.start()
    slots[...] = jnp.zeros_like(slots)
    for at in range((groups + 2) * HALF):
        labels[at] = -1
    copies[0].wait()
    places = []
    for k in range(entries):
        base = (margin[0, k] + 1) * HALF
        row = margin[1, k]
        first = labels[base]
        later = jnp.logical_and(first >= 0, first != row).astype(jnp.int32)
        labels[base + later] = row
        places.append(base + later)
    copies[1].wait()
    copies[2].wait()
    for j, (lo, hi) in enumerate(zip(cuts, cuts[1:])):
        chunks[j].wait()
        parts = [
            lax.dot_general(
                sources[ids[k]], weights[k], (((1,), (1,)), ((), ())), preferred_element_type=jnp.float32
            )
            for k in range(lo, hi)
        ]
        for k in range(lo, hi):
            slots[places[k]] += parts[k - lo]
    copies[3].wait()
    me = lax.axis_index("comp")
    lane = lane_ids(levels)
    lane8 = lane_ids(8)
    packed = jnp.zeros((8, LANES), jnp.float32)
    for g in range(helm.shape[0] // 8):
        at = HELM + 2 * g
        turned = pltpu.roll(helm[8 * g : 8 * g + 8, :], at + 1, 1)
        packed = jnp.where((lane8 == at) | (lane8 == at + 1), turned, packed)
    packed = jnp.concatenate([packed, jnp.zeros((levels - 8, LANES), jnp.float32)], axis=0)
    for step in range(groups):
        to, _ = peer_of(me, step, groups)
        base = (to + 1) * HALF
        out = messages[step]
        out[0] = slots[base]
        out[1] = slots[base + 1]
        before, after = base - HALF, base + HALF
        side = jnp.where(lane < 2, slots[after], packed)
        side = jnp.where(lane >= LANES - 2, slots[before], side)
        side = jnp.where((lane >= 2) & (lane < 4), pltpu.roll(slots[after + 1], 2, 1), side)
        side = jnp.where(
            (lane >= LANES - 4) & (lane < LANES - 2), pltpu.roll(slots[before + 1], LANES - 2, 1), side
        )
        for j, at in enumerate((base, base + 1, before, before + 1, after, after + 1)):
            side = jnp.where(lane == LABEL + j, labels[at].astype(jnp.float32), side)
        out[2] = side


def unpack(messages):
    levels = messages[0].shape[1]
    lane = lane_ids(levels)
    blocks, tags, cols, col_tags = [], [], [], []
    for got in messages:
        side = got[2]
        tag = lambda j: jnp.broadcast_to(side[:, LABEL + j : LABEL + j + 1], side.shape)
        blocks += [got[0], got[1]]
        tags += [tag(0), tag(1)]
        edge = (lane < 2) | (lane >= LANES - 2)
        inner = jnp.where(lane < LANES // 2, pltpu.roll(side, LANES - 2, 1), pltpu.roll(side, 2, 1))
        cols += [jnp.where(edge, side, 0.0), jnp.where(edge, inner, 0.0)]
        col_tags += [jnp.where(lane < LANES // 2, tag(4), tag(2)), jnp.where(lane < LANES // 2, tag(5), tag(3))]

    def cells(row):
        return total([jnp.where(t == float(row), b, 0.0) for t, b in zip(tags, blocks)])

    def beside(row):
        return total([jnp.where(t == float(row), b, 0.0) for t, b in zip(col_tags, cols)])

    return cells, beside


def edge_kernel(helm, *rest):
    messages, (swap_a, swap_b) = rest[:-2], rest[-2:]
    rows, levels = helm.shape[0], messages[0].shape[1]
    cells, beside = unpack(messages)
    lane8 = lane_ids(8)

    def message(edge, beyond):
        x, out = cells(edge), beside(edge)
        image = across(helm[edge : edge + 1, :], x, out) - cells(beyond)
        corner = out[:8]
        for g in range(1, levels // 8):
            turned = pltpu.roll(out[8 * g : 8 * g + 8], 2 * g, 1)
            corner = jnp.where((lane8 == 2 * g - 1) | (lane8 == 2 * g), turned, corner)
        return x, image, corner

    low, high = message(0, 1), message(rows - 1, rows - 2)
    even = lax.rem(lax.axis_index("dom"), 2) == 0
    at = 0
    for a, b in zip(low, high):
        to = pl.ds(at, a.shape[0])
        swap_a[to] = jnp.where(even, b, a)
        swap_b[to] = jnp.where(even, a, b)
        at += a.shape[0]


def inner_kernel(groups, helm, *rest):
    messages, (field, outer, helm_outer, image, second, sums) = rest[:groups], rest[groups:]
    rows, levels, _ = field.shape
    me, comps = lax.axis_index("comp"), lax.axis_size("comp")
    lane, lane8 = lane_ids(levels), lane_ids(8)
    for g in range(rows // 8):
        helm_outer[8 * g : 8 * g + 8, :] = jnp.zeros((8, LANES), jnp.float32)
    for step in range(1, groups):
        _, source = peer_of(me, step, groups)
        top = messages[step][2, :8, :]
        mine = ((lane8 == LANES - 1) & (source == me - 1)) | ((lane8 == 0) & (source == me + 1))
        for g in range(rows // 8):
            at = pl.ds(8 * g, 8)
            turned = pltpu.roll(top, LANES - (HELM + 2 * g + 1), 1)
            helm_outer[at, :] = jnp.where(mine, turned, helm_outer[at, :])
    cells, beside = unpack(messages)
    for i in range(rows):
        field[i] = cells(i)
        outer[i] = beside(i)
    inside = ((lane == LANES - 1) & (me > 0)) | ((lane == 0) & (me < comps - 1))
    for i in range(1, rows - 1):
        x = field[i]
        image[i] = across(helm[i : i + 1, :], x, outer[i]) - (field[i - 1] + field[i + 1])
    parts = [jnp.zeros((levels, LANES), jnp.float32) for _ in range(4)]
    for i in range(rows):
        x = field[i]
        parts[0] = parts[0] + x * x
        if 0 < i < rows - 1:
            u = image[i]
            parts[1] = parts[1] + x * u
            parts[2] = parts[2] + u * u
        if 1 < i < rows - 2:
            out = across(helm_outer[i : i + 1, :], outer[i], x) - (outer[i - 1] + outer[i + 1])
            out = jnp.where(inside, out, 0.0)
            z = across(helm[i : i + 1, :], u, out) - (image[i - 1] + image[i + 1])
            second[i] = z
            parts[3] = parts[3] + u * z
    for j in range(4):
        sums[j] = parts[j]


def rim_kernel(helm, helm_outer, field, outer, image, sums, got_a, got_b, image_rim, second_rim, partial):
    rows, levels, _ = field.shape
    comp, comps = lax.axis_index("comp"), lax.axis_size("comp")
    dom, doms = lax.axis_index("dom"), lax.axis_size("dom")
    even = lax.rem(dom, 2) == 0
    lane = lane_ids(levels)
    inside = ((lane == LANES - 1) & (comp > 0)) | ((lane == 0) & (comp < comps - 1))
    parts = [sums[j] for j in range(4)]
    for side in range(2):
        low = side == 0
        from_b = even if low else jnp.logical_not(even)
        there = dom > 0 if low else dom < doms - 1
        row = (lambda i: i) if low else (lambda i: rows - 1 - i)

        def halo(start, size):
            at = pl.ds(start, size)
            return jnp.where(there, jnp.where(from_b, got_b[at], got_a[at]), 0.0)

        next_row, next_image, corner = halo(0, levels), halo(levels, levels), halo(2 * levels, 8)
        corners = [corner] + [pltpu.roll(corner, LANES - 2 * g, 1) for g in range(1, levels // 8)]
        next_outer = jnp.concatenate(corners, axis=0)
        h = lambda i: helm[row(i) : row(i) + 1, :]
        r = lambda i: field[row(i)]
        e = lambda i: outer[row(i)]
        ho = lambda i: helm_outer[row(i) : row(i) + 1, :]
        beyond = next_image - jnp.where(there, r(0), 0.0)
        u0 = across(h(0), r(0), e(0)) - (next_row + r(1))
        u1, u2 = image[row(1)], image[row(2)]
        out0 = jnp.where(inside, across(ho(0), e(0), r(0)) - (next_outer + e(1)), 0.0)
        out1 = jnp.where(inside, across(ho(1), e(1), r(1)) - (e(0) + e(2)), 0.0)
        z0 = across(h(0), u0, out0) - (beyond + u1)
        z1 = across(h(1), u1, out1) - (u0 + u2)
        image_rim[side] = u0
        second_rim[2 * side] = z0
        second_rim[2 * side + 1] = z1
        parts[1] = parts[1] + r(0) * u0
        parts[2] = parts[2] + u0 * u0
        parts[3] = parts[3] + (u0 * z0 + u1 * z1)
    stacked = jnp.concatenate(parts + [jnp.zeros((LANES - 4 * levels, LANES), jnp.float32)], axis=0)
    line = jnp.sum(stacked.T, axis=0, keepdims=True)
    for d in range(partial.shape[0]):
        partial[d] = line


def final_kernel(partials, field, image, second, image_rim, second_rim, solution_out, residual_out, solution, residual, sems):
    rows, levels, _ = field.shape
    lines = [partials[d] for d in range(partials.shape[0])]
    line = total(lines)
    lane = lane_ids(levels)
    level = lax.broadcasted_iota(jnp.int32, (levels, LANES), 0)
    rr, p, q, s = [
        jnp.sum(jnp.where(lane == level + j * levels, line, 0.0), axis=1, keepdims=True) for j in range(4)
    ]
    mean = p / rr
    square = q / rr
    spread = square - mean * mean
    third = s / rr - mean * (3.0 * square - 2.0 * mean * mean)
    along = SHIFT + mean
    a0 = 1.0 / along
    beta = a0 * a0 * spread
    a1 = 1.0 / (third / spread + along - a0 * spread)
    c1 = 1.0 + beta - SHIFT * a0
    coefs = (
        a0 + a1 * c1,
        -a1 * a0,
        1.0 - SHIFT * a0 - SHIFT * a1 * c1,
        -a0 - a1 * (c1 - SHIFT * a0),
        a1 * a0,
    )
    copies = []
    for g in range(levels // 8):
        part = slice(8 * g, 8 * g + 8)
        sol_r, sol_u, res_r, res_u, res_z = [jnp.broadcast_to(c[part], (8, LANES)) for c in coefs]
        for i in range(rows):
            x = field[i, part, :]
            u = image_rim[0 if i == 0 else 1, part, :] if i in (0, rows - 1) else image[i, part, :]
            rim = {0: 0, 1: 1, rows - 1: 2, rows - 2: 3}.get(i)
            z = second[i, part, :] if rim is None else second_rim[rim, part, :]
            at = pl.ds(8 * g * rows + i, 8, stride=rows)
            solution[at, :] = sol_r * x + sol_u * u
            residual[at, :] = (res_r * x + res_u * u) + res_z * z
        at = pl.ds(8 * g * rows, 8 * rows)
        for j, (src, dst) in enumerate(((solution, solution_out), (residual, residual_out))):
            copies.append(pltpu.make_async_copy(src.at[at], dst.at[at], sems.at[2 * g + j]))
            copies[-1].start()
    for copy in copies:
        copy.wait()


def per_device(source_field, source_block, margin, remap_weight, helm):
    sources, weights = source_field[0, 0], remap_weight[0, 0]
    ids, marks = source_block[0, 0], margin[0, 0].T
    groups, doms = lax.axis_size("comp"), lax.axis_size("dom")
    levels = sources.shape[1]
    rows = helm.shape[0]
    f32 = lambda *shape: jax.ShapeDtypeStruct(shape, jnp.float32)
    slots = (groups + 2) * HALF
    messages = call(
        functools.partial(pack_kernel, groups),
        [f32(3, levels, LANES)] * groups,
        [HBM] * 5,
        [
            pltpu.VMEM((slots, levels, LANES), jnp.float32),
            pltpu.SMEM((slots,), jnp.int32),
            pltpu.SMEM(ids.shape, jnp.int32),
            pltpu.SMEM(marks.shape, jnp.int32),
            pltpu.VMEM(sources.shape, sources.dtype),
            pltpu.VMEM(weights.shape, weights.dtype),
            pltpu.VMEM(helm.shape, helm.dtype),
            pltpu.SemaphoreType.DMA((4 + CHUNKS,)),
        ],
        name="pack",
    )(ids, marks, sources, weights, helm)
    arrived = [messages[0]]
    for step in range(1, groups):
        if groups & (groups - 1) == 0:
            pairs = [(c, c ^ step) for c in range(groups)]
        else:
            pairs = [(c, (c + step) % groups) for c in range(groups)]
        arrived.append(lax.ppermute(messages[step], "comp", pairs))
    swap = f32(2 * levels + 8, LANES)
    swap_a, swap_b = call(edge_kernel, [swap, swap], [VMEM] * (1 + groups), name="edge")(helm, *arrived)

    def pairing(beside):
        pairs = []
        for c in range(groups):
            for d in range(doms):
                e = beside(d)
                there = (c, e) if 0 <= e < doms else (c ^ 1, d)
                if there[0] < groups:
                    pairs.append((c * doms + d, there[0] * doms + there[1]))
        return pairs

    got_a = lax.ppermute(swap_a, ("comp", "dom"), pairing(lambda d: d ^ 1))
    got_b = lax.ppermute(swap_b, ("comp", "dom"), pairing(lambda d: ((d + 1) ^ 1) - 1))
    cube, rim = f32(rows, levels, LANES), f32(2, levels, LANES)
    field, outer, helm_outer, image, second, sums = call(
        functools.partial(inner_kernel, groups),
        [cube, cube, f32(rows, LANES), cube, cube, f32(4, levels, LANES)],
        [VMEM] * (1 + groups),
        name="inner",
        flops=60 * rows * levels * LANES,
    )(helm, *arrived)
    image_rim, second_rim, partial = call(
        rim_kernel,
        [rim, f32(4, levels, LANES), f32(groups * doms, 1, LANES)],
        [VMEM] * 8,
        name="rim",
    )(helm, helm_outer, field, outer, image, sums, got_a, got_b)
    partials = lax.all_to_all(partial, ("comp", "dom"), split_axis=0, concat_axis=0, tiled=True)
    flat = f32(levels * rows, LANES)
    outs = call(
        final_kernel,
        [flat, flat],
        [VMEM] * 6,
        [pltpu.VMEM(flat.shape, flat.dtype)] * 2 + [pltpu.SemaphoreType.DMA((levels // 4,))],
        name="final",
        out_spec=HBM,
    )(partials, field, image, second, image_rim, second_rim)
    return tuple(out.reshape(levels, rows, LANES) for out in outs)


def solution(mesh):
    placed = (
        P("comp", "dom", None, None, None),
        P("comp", "dom", None),
        P("comp", "dom", None, None),
        P("comp", "dom", None, None, None),
        P("dom", "comp"),
    )
    return jax.shard_map(
        per_device,
        mesh=mesh,
        in_specs=placed,
        out_specs=(P(None, "dom", "comp"), P(None, "dom", "comp")),
        check_vma=False,
    )
```

time: 34.7 us -> 31.4 us (0.905)
  blocking collectives: 15.4 us -> 13.5 us
  waiting for transfers between devices: 4.94 us -> 3.39 us
  Pallas kernels: 4.75 us -> 5.52 us
  starting transfers between devices: 5.38 us -> 4.74 us
    all_to_all x1, blocking collectives: 15.4 us -> 13.5 us  [per_device(): lax.all_to_all(partial, ('comp', 'dom'), split_axis=0, concat_axis=0, til...]
    ppermute x2, waiting for transfers between devices: 1.73 us -> 0.18 us  [the longest x1 0.18 us: per_device(): got_a = lax.ppermute(swap_a, ('comp', 'dom'), pairing(lambda d: d ^ 1))]
    pallas_call x1, Pallas kernels: 0.97 us -> 1.69 us  [per_device(): call(functools.partial(pack_kernel, groups), [f32(3, levels, LANES)] * gr...]
    ppermute x2, starting transfers between devices: 2.2 us -> 1.56 us  [the longest x1 1.56 us: per_device(): got_a = lax.ppermute(swap_a, ('comp', 'dom'), pairing(lambda d: d ^ 1))]
    pallas_call x3 -> x4, Pallas kernels: 3.78 us -> 3.82 us  [the longest x1 2.11 us: per_device(): call(functools.partial(inner_kernel, groups), [cube, cube, f32(rows, LANE...]
  transfers between devices with their start and end apart: 5 -> 5, of which waited for: 3 -> 3; matrix products, arithmetic and copies ran while one was open for 0% -> 0% of each run, Pallas kernels for 0% -> 7%
where the time goes in v2:
time: 31.4 us; the launch traced here: 31.1 us
  blocking collectives  13.5 us (43%)
  Pallas kernels  5.52 us (18%)
  starting transfers between devices  4.74 us (15%)
  waiting for transfers between devices  3.39 us (11%)
  local copies, waits for them, and re-layouts  3.29 us (10%)
  between operations  0.68 us (2%)
    all_to_all x1, blocking collectives, per_device(): lax.all_to_all(partial, ('comp', 'dom'), split_axis=0, concat_axis=0, til...  13.5 us
    unnamed x12, local copies, waits for them, and re-layouts  3.29 us
    ppermute x3, waiting for transfers between devices, per_device(): arrived.append(lax.ppermute(messages[step], 'comp', pairs))  3.21 us
    ppermute x3, starting transfers between devices, per_device(): arrived.append(lax.ppermute(messages[step], 'comp', pairs))  3.18 us
    pallas_call x1, Pallas kernels, per_device(): call(functools.partial(inner_kernel, groups), [cube, cube, f32(rows, LANE...  2.11 us
    pallas_call x1, Pallas kernels, per_device(): call(functools.partial(pack_kernel, groups), [f32(3, levels, LANES)] * gr...  1.69 us
    ppermute x1, starting transfers between devices, per_device(): got_a = lax.ppermute(swap_a, ('comp', 'dom'), pairing(lambda d: d ^ 1))  1.56 us
    pallas_call x1, Pallas kernels, per_device(): call(final_kernel, [flat, flat], [VMEM] * 6, [pltpu.VMEM(flat.shape, flat...  1.21 us
  transfers between devices with their start and end apart: 5, of which 3 were waited for; matrix products, arithmetic and copies ran while one was open for 0% of the time, Pallas kernels for 7%

profile of v2, /device:TPU:0, one launch (start us, length us, event | category | flops | bytes accessed | tf_op | source)
XLA Modules:
  0.0 31.1 jit_solution(1481517852779216354)
XLA Ops:
  0.6 0.0 copy-start.4
  0.6 0.0 copy-start.5
  0.7 0.7 %copy-done.4 = s32[1,1,12,2]{2,3,1,0:T(2,128)S(1)} copy-done((s32[1,1,12,2]{2,3,1,0:T(2,128)S(1)}, s32[1,1,12,2]{2,3,1,0:T(2,128)}, u32[]{:S(2)}) %copy-start.4) | copy-done | bytes 120
  1.3 0.0 copy-done.5
  1.3 0.0 copy-start
  1.3 1.0 %copy-done = bf16[1,1,12,128,128]{4,3,2,1,0:T(8,128)(2,1)S(1)} copy-done((bf16[1,1,12,128,128]{4,3,2,1,0:T(8,128)(2,1)S(1)}, bf16[1,1,12,128,128]{4,3,2,1,0:T(8,128)(2,1)}, u32[]{:S(2)}) %copy-start) | copy-done | bytes 393240
  2.3 0.0 copy-start.1
  2.3 0.7 %copy-done.1 = f32[32,128]{1,0:T(8,128)S(1)} copy-done((f32[32,128]{1,0:T(8,128)S(1)}, f32[32,128]{1,0:T(8,128)}, u32[]{:S(2)}) %copy-start.1) | copy-done | bytes 16408
  3.0 0.0 copy-start.3
  3.0 0.9 %copy-done.3 = bf16[1,1,32,16,128]{4,3,2,1,0:T(8,128)(2,1)S(1)} copy-done((bf16[1,1,32,16,128]{4,3,2,1,0:T(8,128)(2,1)S(1)}, bf16[1,1,32,16,128]{4,3,2,1,0:T(8,128)(2,1)}, u32[]{:S(2)}) %copy-start.3) | copy-done | bytes 131096
  3.9 1.7 %pack.1 = (f32[3,16,128]{2,1,0:T(8,128)S(1)}, f32[3,16,128]{2,1,0:T(8,128)S(1)}, f32[3,16,128]{2,1,0:T(8,128)S(1)}, f32[3,16,128]{2,1,0:T(8,128)S(1)}) custom-call(s32[12]{0:T(128)S(1)} %bitcast.11, s32[2,12]{1,0:T(2,128)S(1)} %bitcast.10, bf16[32,16,128]{2,1,0:T(8,128)(2,1)S(1)} %bitcast.9, bf16[12,128,128]{2,1,0:T(8,128)(2,1)S(1)} %bitcast.8, ...), custom_call_target="tpu_custom_call" | custom-call | tf_op jit(solution)/shard_map/pack/pallas_call | solution.py:315
  5.6 0.6 %collective-permute-start = (f32[3,16,128]{2,1,0:T(8,128)S(1)}, f32[3,16,128]{2,1,0:T(8,128)S(1)}, u32[]{:S(2)}, u32[]{:S(2)}) collective-permute-start(f32[3,16,128]{2,1,0:T(8,128)S(1)} %get-tuple-element.20), channel_id=1, source_target_pairs={{0,8},{8,0},{16,24},{24,16},{1,9},{9,1},{17,25},{25,17},{2,10},{10... | collective-permute-start | bytes 73736 | tf_op jit(solution)/shard_map/ppermute | solution.py:337
  6.2 2.6 %collective-permute-start.1 = (f32[3,16,128]{2,1,0:T(8,128)S(1)}, f32[3,16,128]{2,1,0:T(8,128)S(1)}, u32[]{:S(2)}, u32[]{:S(2)}) collective-permute-start(f32[3,16,128]{2,1,0:T(8,128)S(1)} %get-tuple-element.21), channel_id=1, source_target_pairs={{0,16},{8,24},{16,0},{24,8},{1,17},{9,25},{17,1},{25,9},{2,18},{10... | collective-permute-start | bytes 73736 | tf_op jit(solution)/shard_map/ppermute | solution.py:337
  8.8 0.0 collective-permute-start.2
  8.8 0.0 collective-permute-done.rest_1_
  8.8 1.8 %collective-permute-done.1.rest_2_ = f32[3,16,128]{2,1,0:T(8,128)S(1)} collective-permute-done((f32[3,16,128]{2,1,0:T(8,128)S(1)}, f32[3,16,128]{2,1,0:T(8,128)S(1)}, u32[]{:S(2)}, u32[]{:S(2)}) %collective-permute-start.1) | collective-permute-done | bytes 24608 | tf_op jit(solution)/shard_map/ppermute | solution.py:337
  10.6 1.4 %collective-permute-done.2.rest_3_ = f32[3,16,128]{2,1,0:T(8,128)S(1)} collective-permute-done((f32[3,16,128]{2,1,0:T(8,128)S(1)}, f32[3,16,128]{2,1,0:T(8,128)S(1)}, u32[]{:S(2)}, u32[]{:S(2)}) %collective-permute-start.2) | collective-permute-done | bytes 24608 | tf_op jit(solution)/shard_map/ppermute | solution.py:337
  12.0 0.0 copy-start.2
  12.0 0.2 edge.1
  12.3 1.6 %collective-permute-start.3 = (f32[40,128]{1,0:T(8,128)S(1)}, f32[40,128]{1,0:T(8,128)S(1)}, u32[]{:S(2)}, u32[]{:S(2)}) collective-permute-start(f32[40,128]{1,0:T(8,128)S(1)} %get-tuple-element.28), channel_id=1, source_target_pairs={{0,1},{1,0},{2,3},{3,2},{4,5},{5,4},{6,7},{7,6},{8,9},{9,8},{10,11... | collective-permute-start | bytes 61448 | tf_op jit(solution)/shard_map/ppermute | solution.py:351
  13.8 0.0 collective-permute-start.4
  13.8 0.0 copy-done.2
  13.8 2.1 %inner.1 = (f32[32,16,128]{2,1,0:T(8,128)S(1)}, f32[32,16,128]{2,1,0:T(8,128)S(1)}, f32[32,128]{1,0:T(8,128)S(1)}, f32[32,16,128]{2,1,0:T(8,128)S(1)}, f32[32,16...) custom-call(f32[32,128]{1,0:T(8,128)S(1)} %copy-done.2, f32[3,16,128]{2,1,0:T(8,128)S(1)} %get-tuple-element.19.rest_0_, ...), custom_call_target="tpu_custom_call" | custom-call | flops 3932160 | bytes 491520 | tf_op jit(solution)/shard_map/inner/pallas_call | solution.py:354
  15.9 0.2 collective-permute-done.3.got_a
  16.1 0.0 collective-permute-done.4.got_b
  16.1 0.3 rim.1
  16.4 13.5 %all_to_all.5.partials = f32[32,1,128]{2,1,0:T(1,128)S(1)} all-to-all(f32[32,1,128]{2,1,0:T(1,128)S(1)} %get-tuple-element.30), channel_id=1, replica_groups=mesh['comp'=4,'dom'=8] {'comp','dom'}, dimensions={0} | all-to-all | bytes 32768 | tf_op jit(solution)/shard_map/all_to_all | solution.py:367
  29.9 1.2 %final.1 = (f32[512,128]{1,0:T(8,128)}, f32[512,128]{1,0:T(8,128)}) custom-call(f32[32,1,128]{2,1,0:T(1,128)S(1)} %all_to_all.5.partials, f32[32,16,128]{2,1,0:T(8,128)S(1)} %get-tuple-element.24.field, f32[32,16,128]{2,1,0:T(8,128)S(1)} %get-tuple-element.26.image, f32[32,16,128]{2,1,0:T(8,128)S(1)} %get-tuple-element.31.second, ...), custom_call_target="tpu_custom_call" | custom-call | tf_op jit(solution)/shard_map/final/pallas_call | solution.py:369
Async XLA Ops:
  0.6 0.7 %copy-start.4 = (s32[1,1,12,2]{2,3,1,0:T(2,128)S(1)}, s32[1,1,12,2]{2,3,1,0:T(2,128)}, u32[]{:S(2)}) copy-start(s32[1,1,12,2]{2,3,1,0:T(2,128)} %param.7) | copy-start | bytes 292
  0.6 0.7 %copy-start.5 = (s32[1,1,12]{2,1,0:T(1,128)S(1)}, s32[1,1,12]{2,1,0:T(1,128)}, u32[]{:S(2)}) copy-start(s32[1,1,12]{2,1,0:T(1,128)} %param.6) | copy-start | bytes 148
  1.3 1.0 %copy-start = (bf16[1,1,12,128,128]{4,3,2,1,0:T(8,128)(2,1)S(1)}, bf16[1,1,12,128,128]{4,3,2,1,0:T(8,128)(2,1)}, u32[]{:S(2)}) copy-start(bf16[1,1,12,128,128]{4,3,2,1,0:T(8,128)(2,1)} %param.8) | copy-start | bytes 1179652
  2.3 0.7 %copy-start.1 = (f32[32,128]{1,0:T(8,128)S(1)}, f32[32,128]{1,0:T(8,128)}, u32[]{:S(2)}) copy-start(f32[32,128]{1,0:T(8,128)} %helm.5) | copy-start | bytes 49156
  3.0 0.9 %copy-start.3 = (bf16[1,1,32,16,128]{4,3,2,1,0:T(8,128)(2,1)S(1)}, bf16[1,1,32,16,128]{4,3,2,1,0:T(8,128)(2,1)}, u32[]{:S(2)}) copy-start(bf16[1,1,32,16,128]{4,3,2,1,0:T(8,128)(2,1)} %param.5) | copy-start | bytes 393220
  5.6 3.2 %collective-permute-start = (f32[3,16,128]{2,1,0:T(8,128)S(1)}, f32[3,16,128]{2,1,0:T(8,128)S(1)}, u32[]{:S(2)}, u32[]{:S(2)}) collective-permute-start(f32[3,16,128]{2,1,0:T(8,128)S(1)} %get-tuple-element.20), channel_id=1, source_target_pairs={{0,8},{8,0},{16,24},{24,16},{1,9},{9,1},{17,25},{25,17},{2,10},{10... | collective-permute-start | bytes 73736 | tf_op jit(solution)/shard_map/ppermute | solution.py:337
  6.2 4.4 %collective-permute-start.1 = (f32[3,16,128]{2,1,0:T(8,128)S(1)}, f32[3,16,128]{2,1,0:T(8,128)S(1)}, u32[]{:S(2)}, u32[]{:S(2)}) collective-permute-start(f32[3,16,128]{2,1,0:T(8,128)S(1)} %get-tuple-element.21), channel_id=1, source_target_pairs={{0,16},{8,24},{16,0},{24,8},{1,17},{9,25},{17,1},{25,9},{2,18},{10... | collective-permute-start | bytes 73736 | tf_op jit(solution)/shard_map/ppermute | solution.py:337
  8.8 3.3 %collective-permute-start.2 = (f32[3,16,128]{2,1,0:T(8,128)S(1)}, f32[3,16,128]{2,1,0:T(8,128)S(1)}, u32[]{:S(2)}, u32[]{:S(2)}) collective-permute-start(f32[3,16,128]{2,1,0:T(8,128)S(1)} %get-tuple-element.22), channel_id=1, source_target_pairs={{0,24},{8,16},{16,8},{24,0},{1,25},{9,17},{17,9},{25,1},{2,26},{10... | collective-permute-start | bytes 73736 | tf_op jit(solution)/shard_map/ppermute | solution.py:337
  12.0 1.8 %copy-start.2 = (f32[32,128]{1,0:T(8,128)S(1)}, f32[32,128]{1,0:T(8,128)}, u32[]{:S(2)}) copy-start(f32[32,128]{1,0:T(8,128)} %helm.5) | copy-start | bytes 49156
  12.3 3.8 %collective-permute-start.3 = (f32[40,128]{1,0:T(8,128)S(1)}, f32[40,128]{1,0:T(8,128)S(1)}, u32[]{:S(2)}, u32[]{:S(2)}) collective-permute-start(f32[40,128]{1,0:T(8,128)S(1)} %get-tuple-element.28), channel_id=1, source_target_pairs={{0,1},{1,0},{2,3},{3,2},{4,5},{5,4},{6,7},{7,6},{8,9},{9,8},{10,11... | collective-permute-start | bytes 61448 | tf_op jit(solution)/shard_map/ppermute | solution.py:351
  13.8 2.3 %collective-permute-start.4 = (f32[40,128]{1,0:T(8,128)S(1)}, f32[40,128]{1,0:T(8,128)S(1)}, u32[]{:S(2)}, u32[]{:S(2)}) collective-permute-start(f32[40,128]{1,0:T(8,128)S(1)} %get-tuple-element.29), channel_id=1, source_target_pairs={{0,8},{1,2},{2,1},{3,4},{4,3},{5,6},{6,5},{7,15},{8,0},{9,10},{10,... | collective-permute-start | bytes 61448 | tf_op jit(solution)/shard_map/ppermute | solution.py:352

commit v3 on v2

--- a/solution.py
+++ b/solution.py
@@ -17,7 +17,7 @@
 HBM = pl.BlockSpec(memory_space=pltpu.HBM)
 
 
-def call(kernel, out_shape, in_specs, scratch=(), name=None, out_spec=VMEM, flops=0):
+def call(kernel, out_shape, in_specs, scratch=(), name=None, out_spec=VMEM, flops=0, limit=16 * 1024 * 1024):
     return pl.pallas_call(
         kernel,
         out_shape=out_shape,
@@ -25,7 +25,7 @@
         out_specs=jax.tree.map(lambda _: out_spec, out_shape),
         scratch_shapes=scratch,
         name=name,
-        compiler_params=pltpu.CompilerParams(vmem_limit_bytes=16 * 1024 * 1024),
+        compiler_params=pltpu.CompilerParams(vmem_limit_bytes=limit),
         cost_estimate=pl.CostEstimate(flops=flops, bytes_accessed=flops // 8, transcendentals=0) if flops else None,
     )
 
@@ -34,6 +34,10 @@
     if devices & (devices - 1) == 0:
         return me ^ step, me ^ step
     return lax.rem(me + step, devices), lax.rem(me + devices - step, devices)
+
+
+def steps_of(devices):
+    return [*range(0, devices, 2), *range(1, devices, 2)]
 
 
 def lane_ids(rows):
@@ -108,10 +112,9 @@
         turned = pltpu.roll(helm[8 * g : 8 * g + 8, :], at + 1, 1)
         packed = jnp.where((lane8 == at) | (lane8 == at + 1), turned, packed)
     packed = jnp.concatenate([packed, jnp.zeros((levels - 8, LANES), jnp.float32)], axis=0)
-    for step in range(groups):
+    for step, out in zip(steps_of(groups), messages):
         to, _ = peer_of(me, step, groups)
         base = (to + 1) * HALF
-        out = messages[step]
         out[0] = slots[base]
         out[1] = slots[base + 1]
         before, after = base - HALF, base + HALF
@@ -150,7 +153,7 @@
 
 
 def edge_kernel(helm, *rest):
-    messages, (swap_a, swap_b) = rest[:-2], rest[-2:]
+    messages, (swap_b, swap_a) = rest[:-2], rest[-2:]
     rows, levels = helm.shape[0], messages[0].shape[1]
     cells, beside = unpack(messages)
     lane8 = lane_ids(8)
@@ -181,9 +184,9 @@
     lane, lane8 = lane_ids(levels), lane_ids(8)
     for g in range(rows // 8):
         helm_outer[8 * g : 8 * g + 8, :] = jnp.zeros((8, LANES), jnp.float32)
-    for step in range(1, groups):
+    for step, got in list(zip(steps_of(groups), messages))[1:]:
         _, source = peer_of(me, step, groups)
-        top = messages[step][2, :8, :]
+        top = got[2, :8, :]
         mine = ((lane8 == LANES - 1) & (source == me - 1)) | ((lane8 == 0) & (source == me + 1))
         for g in range(rows // 8):
             at = pl.ds(8 * g, 8)
@@ -215,7 +218,7 @@
         sums[j] = parts[j]
 
 
-def rim_kernel(helm, helm_outer, field, outer, image, sums, got_a, got_b, image_rim, second_rim, partial):
+def rim_kernel(helm, helm_outer, field, outer, image, sums, got_b, got_a, image_rim, second_rim, partial):
     rows, levels, _ = field.shape
     comp, comps = lax.axis_index("comp"), lax.axis_size("comp")
     dom, doms = lax.axis_index("dom"), lax.axis_size("dom")
@@ -327,16 +330,16 @@
             pltpu.SemaphoreType.DMA((4 + CHUNKS,)),
         ],
         name="pack",
-    )(ids, marks, sources, weights, helm)
+    )(*[pltpu.with_memory_space_constraint(x, pltpu.HBM) for x in (ids, marks, sources, weights, helm)])
     arrived = [messages[0]]
-    for step in range(1, groups):
+    for step, message in list(zip(steps_of(groups), messages))[1:]:
         if groups & (groups - 1) == 0:
             pairs = [(c, c ^ step) for c in range(groups)]
         else:
             pairs = [(c, (c + step) % groups) for c in range(groups)]
-        arrived.append(lax.ppermute(messages[step], "comp", pairs))
+        arrived.append(lax.ppermute(message, "comp", pairs))
     swap = f32(2 * levels + 8, LANES)
-    swap_a, swap_b = call(edge_kernel, [swap, swap], [VMEM] * (1 + groups), name="edge")(helm, *arrived)
+    swap_b, swap_a = call(edge_kernel, [swap, swap], [VMEM] * (1 + groups), name="edge")(helm, *arrived)
 
     def pairing(beside):
         pairs = []
@@ -348,8 +351,8 @@
                     pairs.append((c * doms + d, there[0] * doms + there[1]))
         return pairs
 
+    got_b = lax.ppermute(swap_b, ("comp", "dom"), pairing(lambda d: ((d + 1) ^ 1) - 1))
     got_a = lax.ppermute(swap_a, ("comp", "dom"), pairing(lambda d: d ^ 1))
-    got_b = lax.ppermute(swap_b, ("comp", "dom"), pairing(lambda d: ((d + 1) ^ 1) - 1))
     cube, rim = f32(rows, levels, LANES), f32(2, levels, LANES)
     field, outer, helm_outer, image, second, sums = call(
         functools.partial(inner_kernel, groups),
@@ -363,7 +366,7 @@
         [rim, f32(4, levels, LANES), f32(groups * doms, 1, LANES)],
         [VMEM] * 8,
         name="rim",
-    )(helm, helm_outer, field, outer, image, sums, got_a, got_b)
+    )(helm, helm_outer, field, outer, image, sums, got_b, got_a)
     partials = lax.all_to_all(partial, ("comp", "dom"), split_axis=0, concat_axis=0, tiled=True)
     flat = f32(levels * rows, LANES)
     outs = call(

time: 31.4 us -> 27.2 us (0.87)
  local copies, waits for them, and re-layouts: 3.29 us -> 0.01 us
  blocking collectives: 13.5 us -> 11.2 us
  starting transfers between devices: 4.74 us -> 6.36 us
  waiting for transfers between devices: 3.39 us -> 3.07 us
    unnamed x12 -> x2, local copies, waits for them, and re-layouts: 3.29 us -> 0.01 us
    all_to_all x1, blocking collectives: 13.5 us -> 11.2 us  [per_device(): lax.all_to_all(partial, ('comp', 'dom'), split_axis=0, concat_axis=0, til...]
    ppermute x1, starting transfers between devices: 1.56 us -> 2.53 us  [per_device(): got_a = lax.ppermute(swap_a, ('comp', 'dom'), pairing(lambda d: d ^ 1))]
    ppermute x1, starting transfers between devices: 0.01 us -> 0.57 us  [per_device(): lax.ppermute(swap_b, ('comp', 'dom'), pairing(lambda d: (d + 1 ^ 1) - 1))]
  transfers between devices with their start and end apart: 5 -> 5, of which waited for: 3 -> 2; matrix products, arithmetic and copies ran while one was open for 0% -> 0% of each run, Pallas kernels for 7% -> 8%
where the time goes in v3:
time: 27.2 us; the launch traced here: 27 us
  blocking collectives  11.2 us (41%)
  starting transfers between devices  6.36 us (23%)
  Pallas kernels  5.7 us (21%)
  waiting for transfers between devices  3.07 us (11%)
  between operations  0.69 us (3%)
    all_to_all x1, blocking collectives, per_device(): lax.all_to_all(partial, ('comp', 'dom'), split_axis=0, concat_axis=0, til...  11.2 us
    ppermute x3, starting transfers between devices, per_device(): arrived.append(lax.ppermute(message, 'comp', pairs))  3.25 us
    ppermute x3, waiting for transfers between devices, per_device(): arrived.append(lax.ppermute(message, 'comp', pairs))  3.06 us
    ppermute x1, starting transfers between devices, per_device(): got_a = lax.ppermute(swap_a, ('comp', 'dom'), pairing(lambda d: d ^ 1))  2.53 us
    pallas_call x1, Pallas kernels, per_device(): call(functools.partial(inner_kernel, groups), [cube, cube, f32(rows, LANE...  2.11 us
    pallas_call x1, Pallas kernels, per_device(): call(functools.partial(pack_kernel, groups), [f32(3, levels, LANES)] * gr...  1.87 us
    pallas_call x1, Pallas kernels, per_device(): call(final_kernel, [flat, flat], [VMEM] * 6, [pltpu.VMEM(flat.shape, flat...  1.21 us
    ppermute x1, starting transfers between devices, per_device(): lax.ppermute(swap_b, ('comp', 'dom'), pairing(lambda d: (d + 1 ^ 1) - 1))  0.57 us
  transfers between devices with their start and end apart: 5, of which 2 were waited for; matrix products, arithmetic and copies ran while one was open for 0% of the time, Pallas kernels for 8%

profile of v3, /device:TPU:0, one launch (start us, length us, event | category | flops | bytes accessed | tf_op | source)
XLA Modules:
  0.0 27.0 jit_solution(9093511547031780261)
XLA Ops:
  0.6 0.0 copy-start
  0.6 1.9 %pack.1 = (f32[3,16,128]{2,1,0:T(8,128)S(1)}, f32[3,16,128]{2,1,0:T(8,128)S(1)}, f32[3,16,128]{2,1,0:T(8,128)S(1)}, f32[3,16,128]{2,1,0:T(8,128)S(1)}) custom-call(s32[12]{0:T(128)} %bitcast.11, s32[2,12]{1,0:T(2,128)} %bitcast.10, bf16[32,16,128]{2,1,0:T(8,128)(2,1)} %bitcast.9, bf16[12,128,128]{2,1,0:T(8,128)(2,1)} %bitcast.8, f32[32,128]{1,0:T(8,128)} %helm.5), custom_call_target="tpu_custom_call" | custom-call | tf_op jit(solution)/shard_map/pack/pallas_call | solution.py:318
  2.5 3.1 %collective-permute-start = (f32[3,16,128]{2,1,0:T(8,128)S(1)}, f32[3,16,128]{2,1,0:T(8,128)S(1)}, u32[]{:S(2)}, u32[]{:S(2)}) collective-permute-start(f32[3,16,128]{2,1,0:T(8,128)S(1)} %get-tuple-element.20), channel_id=1, source_target_pairs={{0,16},{8,24},{16,0},{24,8},{1,17},{9,25},{17,1},{25,9},{2,18},{10... | collective-permute-start | bytes 73736 | tf_op jit(solution)/shard_map/ppermute | solution.py:340
  5.6 0.0 collective-permute-start.1
  5.6 0.2 collective-permute-start.2
  5.8 1.6 %collective-permute-done.rest_1_ = f32[3,16,128]{2,1,0:T(8,128)S(1)} collective-permute-done((f32[3,16,128]{2,1,0:T(8,128)S(1)}, f32[3,16,128]{2,1,0:T(8,128)S(1)}, u32[]{:S(2)}, u32[]{:S(2)}) %collective-permute-start) | collective-permute-done | bytes 24608 | tf_op jit(solution)/shard_map/ppermute | solution.py:340
  7.4 0.0 collective-permute-done.1.rest_2_
  7.4 1.4 %collective-permute-done.2.rest_3_ = f32[3,16,128]{2,1,0:T(8,128)S(1)} collective-permute-done((f32[3,16,128]{2,1,0:T(8,128)S(1)}, f32[3,16,128]{2,1,0:T(8,128)S(1)}, u32[]{:S(2)}, u32[]{:S(2)}) %collective-permute-start.2) | collective-permute-done | bytes 24608 | tf_op jit(solution)/shard_map/ppermute | solution.py:340
  8.8 0.0 copy-done
  8.8 0.2 edge.1
  9.1 0.6 %collective-permute-start.3 = (f32[40,128]{1,0:T(8,128)S(1)}, f32[40,128]{1,0:T(8,128)S(1)}, u32[]{:S(2)}, u32[]{:S(2)}) collective-permute-start(f32[40,128]{1,0:T(8,128)S(1)} %get-tuple-element.28), channel_id=1, source_target_pairs={{0,8},{1,2},{2,1},{3,4},{4,3},{5,6},{6,5},{7,15},{8,0},{9,10},{10,... | collective-permute-start | bytes 61448 | tf_op jit(solution)/shard_map/ppermute | solution.py:354
  9.7 2.5 %collective-permute-start.4 = (f32[40,128]{1,0:T(8,128)S(1)}, f32[40,128]{1,0:T(8,128)S(1)}, u32[]{:S(2)}, u32[]{:S(2)}) collective-permute-start(f32[40,128]{1,0:T(8,128)S(1)} %get-tuple-element.29), channel_id=1, source_target_pairs={{0,1},{1,0},{2,3},{3,2},{4,5},{5,4},{6,7},{7,6},{8,9},{9,8},{10,11... | collective-permute-start | bytes 61448 | tf_op jit(solution)/shard_map/ppermute | solution.py:355
  12.2 2.1 %inner.1 = (f32[32,16,128]{2,1,0:T(8,128)S(1)}, f32[32,16,128]{2,1,0:T(8,128)S(1)}, f32[32,128]{1,0:T(8,128)S(1)}, f32[32,16,128]{2,1,0:T(8,128)S(1)}, f32[32,16...) custom-call(f32[32,128]{1,0:T(8,128)S(1)} %copy-done, f32[3,16,128]{2,1,0:T(8,128)S(1)} %get-tuple-element.19.rest_0_, ...), custom_call_target="tpu_custom_call" | custom-call | flops 3932160 | bytes 491520 | tf_op jit(solution)/shard_map/inner/pallas_call | solution.py:357
  14.3 0.0 collective-permute-done.3.got_b
  14.3 0.0 collective-permute-done.4.got_a
  14.3 0.3 %rim.1 = (f32[2,16,128]{2,1,0:T(8,128)S(1)}, f32[4,16,128]{2,1,0:T(8,128)S(1)}, f32[32,1,128]{2,1,0:T(1,128)S(1)}) custom-call(f32[32,128]{1,0:T(8,128)S(1)} %copy-done, f32[32,128]{1,0:T(8,128)S(1)} %get-tuple-element.23.helm_outer, f32[32,16,128]{2,1,0:T(8,128)S(1)} %get-tuple-element.24.field, f32[32,16,128]{2,1,0:T(8,128)S(1)} %get-tuple-element.25.outer, ...), custom_call_target="tpu_custom_call" | custom-call | tf_op jit(solution)/shard_map/rim/pallas_call | solution.py:364
  14.6 11.2 %all_to_all.5.partials = f32[32,1,128]{2,1,0:T(1,128)S(1)} all-to-all(f32[32,1,128]{2,1,0:T(1,128)S(1)} %get-tuple-element.30), channel_id=1, replica_groups=mesh['comp'=4,'dom'=8] {'comp','dom'}, dimensions={0} | all-to-all | bytes 32768 | tf_op jit(solution)/shard_map/all_to_all | solution.py:370
  25.8 1.2 %final.1 = (f32[512,128]{1,0:T(8,128)}, f32[512,128]{1,0:T(8,128)}) custom-call(f32[32,1,128]{2,1,0:T(1,128)S(1)} %all_to_all.5.partials, f32[32,16,128]{2,1,0:T(8,128)S(1)} %get-tuple-element.24.field, f32[32,16,128]{2,1,0:T(8,128)S(1)} %get-tuple-element.26.image, f32[32,16,128]{2,1,0:T(8,128)S(1)} %get-tuple-element.31.second, ...), custom_call_target="tpu_custom_call" | custom-call | tf_op jit(solution)/shard_map/final/pallas_call | solution.py:372
Async XLA Ops:
  0.6 8.2 %copy-start = (f32[32,128]{1,0:T(8,128)S(1)}, f32[32,128]{1,0:T(8,128)}, u32[]{:S(2)}) copy-start(f32[32,128]{1,0:T(8,128)} %helm.5) | copy-start | bytes 49156
  2.5 4.9 %collective-permute-start = (f32[3,16,128]{2,1,0:T(8,128)S(1)}, f32[3,16,128]{2,1,0:T(8,128)S(1)}, u32[]{:S(2)}, u32[]{:S(2)}) collective-permute-start(f32[3,16,128]{2,1,0:T(8,128)S(1)} %get-tuple-element.20), channel_id=1, source_target_pairs={{0,16},{8,24},{16,0},{24,8},{1,17},{9,25},{17,1},{25,9},{2,18},{10... | collective-permute-start | bytes 73736 | tf_op jit(solution)/shard_map/ppermute | solution.py:340
  5.6 1.8 %collective-permute-start.1 = (f32[3,16,128]{2,1,0:T(8,128)S(1)}, f32[3,16,128]{2,1,0:T(8,128)S(1)}, u32[]{:S(2)}, u32[]{:S(2)}) collective-permute-start(f32[3,16,128]{2,1,0:T(8,128)S(1)} %get-tuple-element.21), channel_id=1, source_target_pairs={{0,8},{8,0},{16,24},{24,16},{1,9},{9,1},{17,25},{25,17},{2,10},{10... | collective-permute-start | bytes 73736 | tf_op jit(solution)/shard_map/ppermute | solution.py:340
  5.6 3.3 %collective-permute-start.2 = (f32[3,16,128]{2,1,0:T(8,128)S(1)}, f32[3,16,128]{2,1,0:T(8,128)S(1)}, u32[]{:S(2)}, u32[]{:S(2)}) collective-permute-start(f32[3,16,128]{2,1,0:T(8,128)S(1)} %get-tuple-element.22), channel_id=1, source_target_pairs={{0,24},{8,16},{16,8},{24,0},{1,25},{9,17},{17,9},{25,1},{2,26},{10... | collective-permute-start | bytes 73736 | tf_op jit(solution)/shard_map/ppermute | solution.py:340
  9.1 5.2 %collective-permute-start.3 = (f32[40,128]{1,0:T(8,128)S(1)}, f32[40,128]{1,0:T(8,128)S(1)}, u32[]{:S(2)}, u32[]{:S(2)}) collective-permute-start(f32[40,128]{1,0:T(8,128)S(1)} %get-tuple-element.28), channel_id=1, source_target_pairs={{0,8},{1,2},{2,1},{3,4},{4,3},{5,6},{6,5},{7,15},{8,0},{9,10},{10,... | collective-permute-start | bytes 61448 | tf_op jit(solution)/shard_map/ppermute | solution.py:354
  9.7 4.7 %collective-permute-start.4 = (f32[40,128]{1,0:T(8,128)S(1)}, f32[40,128]{1,0:T(8,128)S(1)}, u32[]{:S(2)}, u32[]{:S(2)}) collective-permute-start(f32[40,128]{1,0:T(8,128)S(1)} %get-tuple-element.29), channel_id=1, source_target_pairs={{0,1},{1,0},{2,3},{3,2},{4,5},{5,4},{6,7},{7,6},{8,9},{9,8},{10,11... | collective-permute-start | bytes 61448 | tf_op jit(solution)/shard_map/ppermute | solution.py:355

commit v4 on v3

--- a/solution.py
+++ b/solution.py
@@ -11,21 +11,23 @@
 LABEL = 8
 HELM = 16
 SHIFT = 4.0
-CHUNKS = 4
+PART = 4
+CHUNKS = 1
 
 VMEM = pl.BlockSpec(memory_space=pltpu.VMEM)
 HBM = pl.BlockSpec(memory_space=pltpu.HBM)
 
 
-def call(kernel, out_shape, in_specs, scratch=(), name=None, out_spec=VMEM, flops=0, limit=16 * 1024 * 1024):
+def call(kernel, out_shape, in_specs, scratch=(), name=None, out_spec=VMEM, flops=0, aliases={}):
     return pl.pallas_call(
         kernel,
         out_shape=out_shape,
         in_specs=in_specs,
         out_specs=jax.tree.map(lambda _: out_spec, out_shape),
         scratch_shapes=scratch,
+        input_output_aliases=aliases,
         name=name,
-        compiler_params=pltpu.CompilerParams(vmem_limit_bytes=limit),
+        compiler_params=pltpu.CompilerParams(vmem_limit_bytes=16 * 1024 * 1024),
         cost_estimate=pl.CostEstimate(flops=flops, bytes_accessed=flops // 8, transcendentals=0) if flops else None,
     )
 
@@ -76,11 +78,15 @@
     for j, (lo, hi) in enumerate(zip(cuts, cuts[1:])):
         at = pl.ds(lo, hi - lo)
         chunks.append(pltpu.make_async_copy(weights_in.at[at], weights.at[at], sems.at[len(copies) + j]))
-    for copy in copies[:3] + chunks + copies[3:]:
+    for copy in copies[:2] + chunks + copies[2:]:
         copy.start()
     slots[...] = jnp.zeros_like(slots)
     for at in range((groups + 2) * HALF):
         labels[at] = -1
+    me = lax.axis_index("comp")
+    lane = lane_ids(levels)
+    lane8 = lane_ids(8)
+    bases = [(peer_of(me, step, groups)[0] + 1) * HALF for step in steps_of(groups)]
     copies[0].wait()
     places = []
     for k in range(entries):
@@ -90,43 +96,39 @@
         later = jnp.logical_and(first >= 0, first != row).astype(jnp.int32)
         labels[base + later] = row
         places.append(base + later)
-    copies[1].wait()
-    copies[2].wait()
-    for j, (lo, hi) in enumerate(zip(cuts, cuts[1:])):
-        chunks[j].wait()
-        parts = [
-            lax.dot_general(
-                sources[ids[k]], weights[k], (((1,), (1,)), ((), ())), preferred_element_type=jnp.float32
-            )
-            for k in range(lo, hi)
-        ]
-        for k in range(lo, hi):
-            slots[places[k]] += parts[k - lo]
     copies[3].wait()
-    me = lax.axis_index("comp")
-    lane = lane_ids(levels)
-    lane8 = lane_ids(8)
     packed = jnp.zeros((8, LANES), jnp.float32)
     for g in range(helm.shape[0] // 8):
         at = HELM + 2 * g
         turned = pltpu.roll(helm[8 * g : 8 * g + 8, :], at + 1, 1)
         packed = jnp.where((lane8 == at) | (lane8 == at + 1), turned, packed)
     packed = jnp.concatenate([packed, jnp.zeros((levels - 8, LANES), jnp.float32)], axis=0)
-    for step, out in zip(steps_of(groups), messages):
-        to, _ = peer_of(me, step, groups)
-        base = (to + 1) * HALF
+    for base, out in zip(bases, messages):
+        side = packed
+        for j in range(3 * HALF):
+            at = base + (j % HALF) + (0, -HALF, HALF)[j // HALF]
+            side = jnp.where(lane == LABEL + j, labels[at].astype(jnp.float32), side)
+        out[2] = side
+    copies[1].wait()
+    copies[2].wait()
+    for chunk in chunks:
+        chunk.wait()
+    parts = [
+        lax.dot_general(sources[ids[k]], weights[k], (((1,), (1,)), ((), ())), preferred_element_type=jnp.float32)
+        for k in range(entries)
+    ]
+    for k in range(entries):
+        slots[places[k]] += parts[k]
+    for base, out in zip(bases, messages):
         out[0] = slots[base]
         out[1] = slots[base + 1]
         before, after = base - HALF, base + HALF
-        side = jnp.where(lane < 2, slots[after], packed)
+        side = jnp.where(lane < 2, slots[after], out[2])
         side = jnp.where(lane >= LANES - 2, slots[before], side)
         side = jnp.where((lane >= 2) & (lane < 4), pltpu.roll(slots[after + 1], 2, 1), side)
-        side = jnp.where(
+        out[2] = jnp.where(
             (lane >= LANES - 4) & (lane < LANES - 2), pltpu.roll(slots[before + 1], LANES - 2, 1), side
         )
-        for j, at in enumerate((base, base + 1, before, before + 1, after, after + 1)):
-            side = jnp.where(lane == LABEL + j, labels[at].astype(jnp.float32), side)
-        out[2] = side
 
 
 def unpack(messages):
@@ -218,7 +220,7 @@
         sums[j] = parts[j]
 
 
-def rim_kernel(helm, helm_outer, field, outer, image, sums, got_b, got_a, image_rim, second_rim, partial):
+def rim_kernel(helm, helm_outer, field, outer, image_in, second_in, sums, got_b, got_a, image, second, partial):
     rows, levels, _ = field.shape
     comp, comps = lax.axis_index("comp"), lax.axis_size("comp")
     dom, doms = lax.axis_index("dom"), lax.axis_size("dom")
@@ -250,9 +252,9 @@
         out1 = jnp.where(inside, across(ho(1), e(1), r(1)) - (e(0) + e(2)), 0.0)
         z0 = across(h(0), u0, out0) - (beyond + u1)
         z1 = across(h(1), u1, out1) - (u0 + u2)
-        image_rim[side] = u0
-        second_rim[2 * side] = z0
-        second_rim[2 * side + 1] = z1
+        image[row(0)] = u0
+        second[row(0)] = z0
+        second[row(1)] = z1
         parts[1] = parts[1] + r(0) * u0
         parts[2] = parts[2] + u0 * u0
         parts[3] = parts[3] + (u0 * z0 + u1 * z1)
@@ -262,10 +264,9 @@
         partial[d] = line
 
 
-def final_kernel(partials, field, image, second, image_rim, second_rim, solution_out, residual_out, solution, residual, sems):
-    rows, levels, _ = field.shape
-    lines = [partials[d] for d in range(partials.shape[0])]
-    line = total(lines)
+def final_kernel(partials, field, image, second, solution_out, residual_out, solution, residual, sems):
+    levels, rows = residual_out.shape[0], residual_out.shape[1]
+    line = total([partials[d] for d in range(partials.shape[0])])
     lane = lane_ids(levels)
     level = lax.broadcasted_iota(jnp.int32, (levels, LANES), 0)
     rr, p, q, s = [
@@ -287,22 +288,21 @@
         -a0 - a1 * (c1 - SHIFT * a0),
         a1 * a0,
     )
+    coefs = [jnp.broadcast_to(c, (levels, LANES)) for c in coefs]
     copies = []
-    for g in range(levels // 8):
-        part = slice(8 * g, 8 * g + 8)
-        sol_r, sol_u, res_r, res_u, res_z = [jnp.broadcast_to(c[part], (8, LANES)) for c in coefs]
-        for i in range(rows):
-            x = field[i, part, :]
-            u = image_rim[0 if i == 0 else 1, part, :] if i in (0, rows - 1) else image[i, part, :]
-            rim = {0: 0, 1: 1, rows - 1: 2, rows - 2: 3}.get(i)
-            z = second[i, part, :] if rim is None else second_rim[rim, part, :]
-            at = pl.ds(8 * g * rows + i, 8, stride=rows)
-            solution[at, :] = sol_r * x + sol_u * u
-            residual[at, :] = (res_r * x + res_u * u) + res_z * z
-        at = pl.ds(8 * g * rows, 8 * rows)
-        for j, (src, dst) in enumerate(((solution, solution_out), (residual, residual_out))):
-            copies.append(pltpu.make_async_copy(src.at[at], dst.at[at], sems.at[2 * g + j]))
-            copies[-1].start()
+    for n in range(levels):
+        sol_r, sol_u, res_r, res_u, res_z = [jnp.broadcast_to(c[n : n + 1], (8, LANES)) for c in coefs]
+        for g in range(rows // 8):
+            at = pl.ds(8 * g * levels + n, 8, stride=levels)
+            x, u, z = field[at, :], image[at, :], second[at, :]
+            to = pl.ds(8 * g, 8)
+            solution[n, to, :] = sol_r * x + sol_u * u
+            residual[n, to, :] = (res_r * x + res_u * u) + res_z * z
+        if (n + 1) % PART == 0:
+            at = pl.ds(n + 1 - PART, PART)
+            for src, dst in ((solution, solution_out), (residual, residual_out)):
+                copies.append(pltpu.make_async_copy(src.at[at], dst.at[at], sems.at[len(copies)]))
+                copies[-1].start()
     for copy in copies:
         copy.wait()
 
@@ -353,7 +353,7 @@
 
     got_b = lax.ppermute(swap_b, ("comp", "dom"), pairing(lambda d: ((d + 1) ^ 1) - 1))
     got_a = lax.ppermute(swap_a, ("comp", "dom"), pairing(lambda d: d ^ 1))
-    cube, rim = f32(rows, levels, LANES), f32(2, levels, LANES)
+    cube = f32(rows, levels, LANES)
     field, outer, helm_outer, image, second, sums = call(
         functools.partial(inner_kernel, groups),
         [cube, cube, f32(rows, LANES), cube, cube, f32(4, levels, LANES)],
@@ -361,23 +361,26 @@
         name="inner",
         flops=60 * rows * levels * LANES,
     )(helm, *arrived)
-    image_rim, second_rim, partial = call(
+    image, second, partial = call(
         rim_kernel,
-        [rim, f32(4, levels, LANES), f32(groups * doms, 1, LANES)],
-        [VMEM] * 8,
+        [cube, cube, f32(groups * doms, 1, LANES)],
+        [VMEM] * 9,
         name="rim",
-    )(helm, helm_outer, field, outer, image, sums, got_b, got_a)
+        aliases={4: 0, 5: 1},
+    )(helm, helm_outer, field, outer, image, second, sums, got_b, got_a)
     partials = lax.all_to_all(partial, ("comp", "dom"), split_axis=0, concat_axis=0, tiled=True)
-    flat = f32(levels * rows, LANES)
-    outs = call(
-        final_kernel,
-        [flat, flat],
-        [VMEM] * 6,
-        [pltpu.VMEM(flat.shape, flat.dtype)] * 2 + [pltpu.SemaphoreType.DMA((levels // 4,))],
-        name="final",
-        out_spec=HBM,
-    )(partials, field, image, second, image_rim, second_rim)
-    return tuple(out.reshape(levels, rows, LANES) for out in outs)
+    whole = f32(levels, rows, LANES)
+    flat = lambda x: x.reshape(rows * levels, LANES)
+    return tuple(
+        call(
+            final_kernel,
+            [whole, whole],
+            [VMEM] * 4,
+            [pltpu.VMEM(whole.shape, whole.dtype)] * 2 + [pltpu.SemaphoreType.DMA((2 * levels // PART,))],
+            name="final",
+            out_spec=HBM,
+        )(partials, flat(field), flat(image), flat(second))
+    )
 
 
 def solution(mesh):

time: 27.2 us -> 26.8 us (0.985)
  Pallas kernels: 5.7 us -> 5.17 us
    pallas_call x1, Pallas kernels: 1.87 us -> 1.48 us  [per_device(): call(functools.partial(pack_kernel, groups), [f32(3, levels, LANES)] * gr...]
where the time goes in v4:
time: 26.8 us; the launch traced here: 26.5 us
  blocking collectives  11.2 us (42%)
  starting transfers between devices  6.36 us (24%)
  Pallas kernels  5.17 us (19%)
  waiting for transfers between devices  3.07 us (11%)
  between operations  0.69 us (3%)
    all_to_all x1, blocking collectives, per_device(): lax.all_to_all(partial, ('comp', 'dom'), split_axis=0, concat_axis=0, til...  11.2 us
    ppermute x3, starting transfers between devices, per_device(): arrived.append(lax.ppermute(message, 'comp', pairs))  3.25 us
    ppermute x3, waiting for transfers between devices, per_device(): arrived.append(lax.ppermute(message, 'comp', pairs))  3.06 us
    ppermute x1, starting transfers between devices, per_device(): got_a = lax.ppermute(swap_a, ('comp', 'dom'), pairing(lambda d: d ^ 1))  2.53 us
    pallas_call x1, Pallas kernels, per_device(): call(functools.partial(inner_kernel, groups), [cube, cube, f32(rows, LANE...  2.1 us
    pallas_call x1, Pallas kernels, per_device(): call(functools.partial(pack_kernel, groups), [f32(3, levels, LANES)] * gr...  1.48 us
    pallas_call x1, Pallas kernels, per_device(): call(final_kernel, [whole, whole], [VMEM] * 4, [pltpu.VMEM(whole.shape, w...  1.08 us
    ppermute x1, starting transfers between devices, per_device(): lax.ppermute(swap_b, ('comp', 'dom'), pairing(lambda d: (d + 1 ^ 1) - 1))  0.57 us
  transfers between devices with their start and end apart: 5, of which 2 were waited for; matrix products, arithmetic and copies ran while one was open for 0% of the time, Pallas kernels for 8%

profile of v4, /device:TPU:0, one launch (start us, length us, event | category | flops | bytes accessed | tf_op | source)
XLA Modules:
  0.0 26.5 jit_solution(2696802410042987713)
XLA Ops:
  0.6 0.0 copy-start
  0.6 1.5 %pack.1 = (f32[3,16,128]{2,1,0:T(8,128)S(1)}, f32[3,16,128]{2,1,0:T(8,128)S(1)}, f32[3,16,128]{2,1,0:T(8,128)S(1)}, f32[3,16,128]{2,1,0:T(8,128)S(1)}) custom-call(s32[12]{0:T(128)} %bitcast.15, s32[2,12]{1,0:T(2,128)} %bitcast.14, bf16[32,16,128]{2,1,0:T(8,128)(2,1)} %bitcast.13, bf16[12,128,128]{2,1,0:T(8,128)(2,1)} %bitcast.12, f32[32,128]{1,0:T(8,128)} %helm.5), custom_call_target="tpu_custom_call" | custom-call | tf_op jit(solution)/shard_map/pack/pallas_call | solution.py:318
  2.1 3.1 %collective-permute-start = (f32[3,16,128]{2,1,0:T(8,128)S(1)}, f32[3,16,128]{2,1,0:T(8,128)S(1)}, u32[]{:S(2)}, u32[]{:S(2)}) collective-permute-start(f32[3,16,128]{2,1,0:T(8,128)S(1)} %get-tuple-element.18), channel_id=1, source_target_pairs={{0,16},{8,24},{16,0},{24,8},{1,17},{9,25},{17,1},{25,9},{2,18},{10... | collective-permute-start | bytes 73736 | tf_op jit(solution)/shard_map/ppermute | solution.py:340
  5.2 0.0 collective-permute-start.1
  5.2 0.2 collective-permute-start.2
  5.4 1.6 %collective-permute-done.rest_1_ = f32[3,16,128]{2,1,0:T(8,128)S(1)} collective-permute-done((f32[3,16,128]{2,1,0:T(8,128)S(1)}, f32[3,16,128]{2,1,0:T(8,128)S(1)}, u32[]{:S(2)}, u32[]{:S(2)}) %collective-permute-start) | collective-permute-done | bytes 24608 | tf_op jit(solution)/shard_map/ppermute | solution.py:340
  7.0 0.0 collective-permute-done.1.rest_2_
  7.0 1.4 %collective-permute-done.2.rest_3_ = f32[3,16,128]{2,1,0:T(8,128)S(1)} collective-permute-done((f32[3,16,128]{2,1,0:T(8,128)S(1)}, f32[3,16,128]{2,1,0:T(8,128)S(1)}, u32[]{:S(2)}, u32[]{:S(2)}) %collective-permute-start.2) | collective-permute-done | bytes 24608 | tf_op jit(solution)/shard_map/ppermute | solution.py:340
  8.5 0.0 copy-done
  8.5 0.2 edge.1
  8.7 0.6 %collective-permute-start.3 = (f32[40,128]{1,0:T(8,128)S(1)}, f32[40,128]{1,0:T(8,128)S(1)}, u32[]{:S(2)}, u32[]{:S(2)}) collective-permute-start(f32[40,128]{1,0:T(8,128)S(1)} %get-tuple-element.27), channel_id=1, source_target_pairs={{0,8},{1,2},{2,1},{3,4},{4,3},{5,6},{6,5},{7,15},{8,0},{9,10},{10,... | collective-permute-start | bytes 61448 | tf_op jit(solution)/shard_map/ppermute | solution.py:354
  9.3 2.5 %collective-permute-start.4 = (f32[40,128]{1,0:T(8,128)S(1)}, f32[40,128]{1,0:T(8,128)S(1)}, u32[]{:S(2)}, u32[]{:S(2)}) collective-permute-start(f32[40,128]{1,0:T(8,128)S(1)} %get-tuple-element.28), channel_id=1, source_target_pairs={{0,1},{1,0},{2,3},{3,2},{4,5},{5,4},{6,7},{7,6},{8,9},{9,8},{10,11... | collective-permute-start | bytes 61448 | tf_op jit(solution)/shard_map/ppermute | solution.py:355
  11.8 2.1 %inner.1 = (f32[32,16,128]{2,1,0:T(8,128)S(1)}, f32[32,16,128]{2,1,0:T(8,128)S(1)}, f32[32,128]{1,0:T(8,128)S(1)}, f32[32,16,128]{2,1,0:T(8,128)S(1)}, f32[32,16...) custom-call(f32[32,128]{1,0:T(8,128)S(1)} %copy-done, f32[3,16,128]{2,1,0:T(8,128)S(1)} %get-tuple-element.17.rest_0_, ...), custom_call_target="tpu_custom_call" | custom-call | flops 3932160 | bytes 491520 | tf_op jit(solution)/shard_map/inner/pallas_call | solution.py:357
  13.9 0.0 collective-permute-done.3.got_b
  13.9 0.0 collective-permute-done.4.got_a
  13.9 0.3 %rim.1 = (f32[32,16,128]{2,1,0:T(8,128)S(1)}, f32[32,16,128]{2,1,0:T(8,128)S(1)}, f32[32,1,128]{2,1,0:T(1,128)S(1)}) custom-call(f32[32,128]{1,0:T(8,128)S(1)} %copy-done, f32[32,128]{1,0:T(8,128)S(1)} %get-tuple-element.21.helm_outer, f32[32,16,128]{2,1,0:T(8,128)S(1)} %get-tuple-element.22.field, ...), custom_call_target="tpu_custom_call", output_to_operand_aliasing={{0}: (4, {}), {1}: (5, {})} | custom-call | tf_op jit(solution)/shard_map/rim/pallas_call | solution.py:364
  14.2 11.2 %all_to_all.5.partials = f32[32,1,128]{2,1,0:T(1,128)S(1)} all-to-all(f32[32,1,128]{2,1,0:T(1,128)S(1)} %get-tuple-element.29), channel_id=1, replica_groups=mesh['comp'=4,'dom'=8] {'comp','dom'}, dimensions={0} | all-to-all | bytes 32768 | tf_op jit(solution)/shard_map/all_to_all | solution.py:371
  25.4 1.1 %final.1 = (f32[16,32,128]{2,1,0:T(8,128)}, f32[16,32,128]{2,1,0:T(8,128)}) custom-call(f32[32,1,128]{2,1,0:T(1,128)S(1)} %all_to_all.5.partials, f32[512,128]{1,0:T(8,128)S(1)} %bitcast.9, f32[512,128]{1,0:T(8,128)S(1)} %bitcast.10, f32[512,128]{1,0:T(8,128)S(1)} %bitcast.11), custom_call_target="tpu_custom_call" | custom-call | tf_op jit(solution)/shard_map/final/pallas_call | solution.py:375
Async XLA Ops:
  0.6 7.8 %copy-start = (f32[32,128]{1,0:T(8,128)S(1)}, f32[32,128]{1,0:T(8,128)}, u32[]{:S(2)}) copy-start(f32[32,128]{1,0:T(8,128)} %helm.5) | copy-start | bytes 49156
  2.1 4.9 %collective-permute-start = (f32[3,16,128]{2,1,0:T(8,128)S(1)}, f32[3,16,128]{2,1,0:T(8,128)S(1)}, u32[]{:S(2)}, u32[]{:S(2)}) collective-permute-start(f32[3,16,128]{2,1,0:T(8,128)S(1)} %get-tuple-element.18), channel_id=1, source_target_pairs={{0,16},{8,24},{16,0},{24,8},{1,17},{9,25},{17,1},{25,9},{2,18},{10... | collective-permute-start | bytes 73736 | tf_op jit(solution)/shard_map/ppermute | solution.py:340
  5.2 1.8 %collective-permute-start.1 = (f32[3,16,128]{2,1,0:T(8,128)S(1)}, f32[3,16,128]{2,1,0:T(8,128)S(1)}, u32[]{:S(2)}, u32[]{:S(2)}) collective-permute-start(f32[3,16,128]{2,1,0:T(8,128)S(1)} %get-tuple-element.19), channel_id=1, source_target_pairs={{0,8},{8,0},{16,24},{24,16},{1,9},{9,1},{17,25},{25,17},{2,10},{10... | collective-permute-start | bytes 73736 | tf_op jit(solution)/shard_map/ppermute | solution.py:340
  5.2 3.3 %collective-permute-start.2 = (f32[3,16,128]{2,1,0:T(8,128)S(1)}, f32[3,16,128]{2,1,0:T(8,128)S(1)}, u32[]{:S(2)}, u32[]{:S(2)}) collective-permute-start(f32[3,16,128]{2,1,0:T(8,128)S(1)} %get-tuple-element.20), channel_id=1, source_target_pairs={{0,24},{8,16},{16,8},{24,0},{1,25},{9,17},{17,9},{25,1},{2,26},{10... | collective-permute-start | bytes 73736 | tf_op jit(solution)/shard_map/ppermute | solution.py:340
  8.7 5.2 %collective-permute-start.3 = (f32[40,128]{1,0:T(8,128)S(1)}, f32[40,128]{1,0:T(8,128)S(1)}, u32[]{:S(2)}, u32[]{:S(2)}) collective-permute-start(f32[40,128]{1,0:T(8,128)S(1)} %get-tuple-element.27), channel_id=1, source_target_pairs={{0,8},{1,2},{2,1},{3,4},{4,3},{5,6},{6,5},{7,15},{8,0},{9,10},{10,... | collective-permute-start | bytes 61448 | tf_op jit(solution)/shard_map/ppermute | solution.py:354
  9.3 4.6 %collective-permute-start.4 = (f32[40,128]{1,0:T(8,128)S(1)}, f32[40,128]{1,0:T(8,128)S(1)}, u32[]{:S(2)}, u32[]{:S(2)}) collective-permute-start(f32[40,128]{1,0:T(8,128)S(1)} %get-tuple-element.28), channel_id=1, source_target_pairs={{0,1},{1,0},{2,3},{3,2},{4,5},{5,4},{6,7},{7,6},{8,9},{9,8},{10,11... | collective-permute-start | bytes 61448 | tf_op jit(solution)/shard_map/ppermute | solution.py:355

commit v5 on v4

--- a/solution.py
+++ b/solution.py
@@ -9,9 +9,11 @@
 HALF = 2
 LANES = 128
 LABEL = 8
+APART = 32
 HELM = 16
 SHIFT = 4.0
 PART = 4
+PAD = 8
 CHUNKS = 1
 
 VMEM = pl.BlockSpec(memory_space=pltpu.VMEM)
@@ -102,13 +104,12 @@
         at = HELM + 2 * g
         turned = pltpu.roll(helm[8 * g : 8 * g + 8, :], at + 1, 1)
         packed = jnp.where((lane8 == at) | (lane8 == at + 1), turned, packed)
-    packed = jnp.concatenate([packed, jnp.zeros((levels - 8, LANES), jnp.float32)], axis=0)
     for base, out in zip(bases, messages):
         side = packed
         for j in range(3 * HALF):
             at = base + (j % HALF) + (0, -HALF, HALF)[j // HALF]
-            side = jnp.where(lane == LABEL + j, labels[at].astype(jnp.float32), side)
-        out[2] = side
+            side = jnp.where(lane8 == LABEL + j, labels[at].astype(jnp.float32), side)
+        out[HALF * levels :] = side
     copies[1].wait()
     copies[2].wait()
     for chunk in chunks:
@@ -120,29 +121,40 @@
     for k in range(entries):
         slots[places[k]] += parts[k]
     for base, out in zip(bases, messages):
-        out[0] = slots[base]
-        out[1] = slots[base + 1]
+        out[0:levels] = slots[base]
+        out[levels : 2 * levels] = slots[base + 1]
         before, after = base - HALF, base + HALF
-        side = jnp.where(lane < 2, slots[after], out[2])
-        side = jnp.where(lane >= LANES - 2, slots[before], side)
-        side = jnp.where((lane >= 2) & (lane < 4), pltpu.roll(slots[after + 1], 2, 1), side)
-        out[2] = jnp.where(
-            (lane >= LANES - 4) & (lane < LANES - 2), pltpu.roll(slots[before + 1], LANES - 2, 1), side
+        cols = jnp.where(lane < LANES // 2, slots[after], slots[before])
+        inner = jnp.where(
+            lane < LANES // 2, pltpu.roll(slots[after + 1], 2, 1), pltpu.roll(slots[before + 1], LANES - 2, 1)
         )
-
-
-def unpack(messages):
-    levels = messages[0].shape[1]
+        cols = jnp.where((lane < 2) | (lane >= LANES - 2), cols, inner)
+        side = out[HALF * levels :]
+        for g in range(levels // 8):
+            turned = cols[8 * g : 8 * g + 8]
+            if g:
+                turned = pltpu.roll(turned, APART * g, 1)
+            here = (lane8 + (LANES - APART * g + 4)) % LANES < 8
+            side = jnp.where(here, turned, side)
+        out[HALF * levels :] = side
+
+
+def side_of(message, levels):
+    side = message[HALF * levels :]
+    turned = [side] + [pltpu.roll(side, LANES - APART * g, 1) for g in range(1, levels // 8)]
+    return side, jnp.concatenate(turned, axis=0)
+
+
+def unpack(messages, levels):
     lane = lane_ids(levels)
     blocks, tags, cols, col_tags = [], [], [], []
     for got in messages:
-        side = got[2]
-        tag = lambda j: jnp.broadcast_to(side[:, LABEL + j : LABEL + j + 1], side.shape)
-        blocks += [got[0], got[1]]
+        side, ends = side_of(got, levels)
+        tag = lambda j: jnp.broadcast_to(side[0:1, LABEL + j : LABEL + j + 1], (levels, LANES))
+        blocks += [got[0:levels], got[levels : 2 * levels]]
         tags += [tag(0), tag(1)]
-        edge = (lane < 2) | (lane >= LANES - 2)
-        inner = jnp.where(lane < LANES // 2, pltpu.roll(side, LANES - 2, 1), pltpu.roll(side, 2, 1))
-        cols += [jnp.where(edge, side, 0.0), jnp.where(edge, inner, 0.0)]
+        inner = jnp.where(lane < LANES // 2, pltpu.roll(ends, LANES - 2, 1), pltpu.roll(ends, 2, 1))
+        cols += [ends, inner]
         col_tags += [jnp.where(lane < LANES // 2, tag(4), tag(2)), jnp.where(lane < LANES // 2, tag(5), tag(3))]
 
     def cells(row):
@@ -156,8 +168,8 @@
 
 def edge_kernel(helm, *rest):
     messages, (swap_b, swap_a) = rest[:-2], rest[-2:]
-    rows, levels = helm.shape[0], messages[0].shape[1]
-    cells, beside = unpack(messages)
+    rows, levels = helm.shape[0], (messages[0].shape[0] - 8) // HALF
+    cells, beside = unpack(messages, levels)
     lane8 = lane_ids(8)
 
     def message(edge, beyond):
@@ -180,59 +192,85 @@
 
 
 def inner_kernel(groups, helm, *rest):
-    messages, (field, outer, helm_outer, image, second, sums) = rest[:groups], rest[groups:]
-    rows, levels, _ = field.shape
+    messages, (field, image, second, sums, outer, helm_outer) = rest[:groups], rest[groups:]
+    rows, levels = helm.shape[0], sums.shape[0] // 4
+    pitch = rows + PAD
     me, comps = lax.axis_index("comp"), lax.axis_size("comp")
     lane, lane8 = lane_ids(levels), lane_ids(8)
-    for g in range(rows // 8):
-        helm_outer[8 * g : 8 * g + 8, :] = jnp.zeros((8, LANES), jnp.float32)
-    for step, got in list(zip(steps_of(groups), messages))[1:]:
-        _, source = peer_of(me, step, groups)
-        top = got[2, :8, :]
-        mine = ((lane8 == LANES - 1) & (source == me - 1)) | ((lane8 == 0) & (source == me + 1))
-        for g in range(rows // 8):
-            at = pl.ds(8 * g, 8)
-            turned = pltpu.roll(top, LANES - (HELM + 2 * g + 1), 1)
-            helm_outer[at, :] = jnp.where(mine, turned, helm_outer[at, :])
-    cells, beside = unpack(messages)
-    for i in range(rows):
-        field[i] = cells(i)
-        outer[i] = beside(i)
-    inside = ((lane == LANES - 1) & (me > 0)) | ((lane == 0) & (me < comps - 1))
-    for i in range(1, rows - 1):
-        x = field[i]
-        image[i] = across(helm[i : i + 1, :], x, outer[i]) - (field[i - 1] + field[i + 1])
-    parts = [jnp.zeros((levels, LANES), jnp.float32) for _ in range(4)]
-    for i in range(rows):
-        x = field[i]
-        parts[0] = parts[0] + x * x
-        if 0 < i < rows - 1:
-            u = image[i]
-            parts[1] = parts[1] + x * u
-            parts[2] = parts[2] + u * u
-        if 1 < i < rows - 2:
-            out = across(helm_outer[i : i + 1, :], outer[i], x) - (outer[i - 1] + outer[i + 1])
-            out = jnp.where(inside, out, 0.0)
-            z = across(helm[i : i + 1, :], u, out) - (image[i - 1] + image[i + 1])
-            second[i] = z
-            parts[3] = parts[3] + u * z
-    for j in range(4):
-        sums[j] = parts[j]
-
-
-def rim_kernel(helm, helm_outer, field, outer, image_in, second_in, sums, got_b, got_a, image, second, partial):
-    rows, levels, _ = field.shape
+    field[...] = jnp.zeros_like(field)
+    outer[...] = jnp.zeros_like(outer)
+    helm_outer[...] = jnp.zeros_like(helm_outer)
+    low, high = lane < 2, lane >= LANES - 2
+    for step, got in zip(steps_of(groups), messages):
+        side, ends = side_of(got, levels)
+
+        def row_of(j):
+            label = side[0:1, LABEL + j : LABEL + j + 1].astype(jnp.int32)[0, 0]
+            return pl.ds(PAD + lax.max(label, 0), levels, stride=pitch)
+
+        turned = (pltpu.roll(ends, LANES - 2, 1), pltpu.roll(ends, 2, 1))
+        for j in range(HALF):
+            field[row_of(j), :] += got[j * levels : (j + 1) * levels]
+            outer[row_of(HALF + j), :] += jnp.where(high, turned[1] if j else ends, 0.0)
+            outer[row_of(2 * HALF + j), :] += jnp.where(low, turned[0] if j else ends, 0.0)
+        if step:
+            _, source = peer_of(me, step, groups)
+            mine = ((lane8 == LANES - 1) & (source == me - 1)) | ((lane8 == 0) & (source == me + 1))
+            for g in range(rows // 8):
+                at = pl.ds(8 * g, 8)
+                helm_outer[at, :] = jnp.where(
+                    mine, pltpu.roll(side, LANES - (HELM + 2 * g + 1), 1), helm_outer[at, :]
+                )
+    inside = ((lane8 == LANES - 1) & (me > 0)) | ((lane8 == 0) & (me < comps - 1))
+    sub = lax.broadcasted_iota(jnp.int32, (8, LANES), 0)
+    for n in range(levels + 1):
+        image[pl.ds(n * pitch, PAD), :] = jnp.zeros((PAD, LANES), jnp.float32)
+
+    def beside(ref, at):
+        return ref[pl.ds(at - 1, 8), :] + ref[pl.ds(at + 1, 8), :]
+
+    def off_rim(x, g, width):
+        if g == 0:
+            x = jnp.where(sub < width, 0.0, x)
+        if g == rows // 8 - 1:
+            x = jnp.where(sub >= 8 - width, 0.0, x)
+        return x
+
+    for n in range(levels):
+        at = [PAD + n * pitch + 8 * g for g in range(rows // 8)]
+        xs = [field[pl.ds(a, 8), :] for a in at]
+        es = [outer[pl.ds(a, 8), :] for a in at]
+        us = [across(helm[8 * g : 8 * g + 8, :], xs[g], es[g]) - beside(field, a) for g, a in enumerate(at)]
+        for a, u in zip(at, us):
+            image[pl.ds(a, 8), :] = u
+        parts = [[], [], [], []]
+        for g, a in enumerate(at):
+            x, e, u = xs[g], es[g], us[g]
+            out = jnp.where(inside, across(helm_outer[8 * g : 8 * g + 8, :], e, x) - beside(outer, a), 0.0)
+            z = across(helm[8 * g : 8 * g + 8, :], u, out) - beside(image, a)
+            second[pl.ds(n * rows + 8 * g, 8), :] = z
+            u1, u2 = off_rim(u, g, 1), off_rim(u, g, 2)
+            for part, a, b in zip(parts, (x, x, u1, u2), (x, u1, u1, z)):
+                part.append(a * b)
+        for j, part in enumerate(parts):
+            sums[pl.ds(j * levels + n, 1), :] = jnp.sum(total(part), axis=0, keepdims=True)
+
+
+def rim_kernel(helm, field, image_in, second_in, sums, got_b, got_a, image, second, partial):
+    rows, levels = helm.shape[0], sums.shape[0] // 4
+    pitch = rows + PAD
     comp, comps = lax.axis_index("comp"), lax.axis_size("comp")
     dom, doms = lax.axis_index("dom"), lax.axis_size("dom")
     even = lax.rem(dom, 2) == 0
     lane = lane_ids(levels)
     inside = ((lane == LANES - 1) & (comp > 0)) | ((lane == 0) & (comp < comps - 1))
-    parts = [sums[j] for j in range(4)]
+    parts = [sums[pl.ds(j * levels, levels), :] for j in range(4)]
     for side in range(2):
-        low = side == 0
-        from_b = even if low else jnp.logical_not(even)
-        there = dom > 0 if low else dom < doms - 1
-        row = (lambda i: i) if low else (lambda i: rows - 1 - i)
+        from_b = even if side == 0 else jnp.logical_not(even)
+        there = dom > 0 if side == 0 else dom < doms - 1
+        first, second_row = (0, 1) if side == 0 else (rows - 1, rows - 2)
+        at0, at1 = pl.ds(PAD + first, levels, stride=pitch), pl.ds(PAD + second_row, levels, stride=pitch)
+        to0, to1 = pl.ds(first, levels, stride=rows), pl.ds(second_row, levels, stride=rows)
 
         def halo(start, size):
             at = pl.ds(start, size)
@@ -240,22 +278,17 @@
 
         next_row, next_image, corner = halo(0, levels), halo(levels, levels), halo(2 * levels, 8)
         corners = [corner] + [pltpu.roll(corner, LANES - 2 * g, 1) for g in range(1, levels // 8)]
-        next_outer = jnp.concatenate(corners, axis=0)
-        h = lambda i: helm[row(i) : row(i) + 1, :]
-        r = lambda i: field[row(i)]
-        e = lambda i: outer[row(i)]
-        ho = lambda i: helm_outer[row(i) : row(i) + 1, :]
-        beyond = next_image - jnp.where(there, r(0), 0.0)
-        u0 = across(h(0), r(0), e(0)) - (next_row + r(1))
-        u1, u2 = image[row(1)], image[row(2)]
-        out0 = jnp.where(inside, across(ho(0), e(0), r(0)) - (next_outer + e(1)), 0.0)
-        out1 = jnp.where(inside, across(ho(1), e(1), r(1)) - (e(0) + e(2)), 0.0)
-        z0 = across(h(0), u0, out0) - (beyond + u1)
-        z1 = across(h(1), u1, out1) - (u0 + u2)
-        image[row(0)] = u0
-        second[row(0)] = z0
-        second[row(1)] = z1
-        parts[1] = parts[1] + r(0) * u0
+        next_outer = jnp.where(inside, jnp.concatenate(corners, axis=0), 0.0)
+        r0, u1 = field[at0, :], image_in[at1, :]
+        u0 = image_in[at0, :] - next_row
+        beyond = next_image - jnp.where(there, r0, 0.0)
+        h = helm[first : first + 1, :]
+        z0 = second_in[to0, :] - (across(h, next_row, next_outer) + beyond)
+        z1 = second_in[to1, :] + next_row
+        image[at0, :] = u0
+        second[to0, :] = z0
+        second[to1, :] = z1
+        parts[1] = parts[1] + r0 * u0
         parts[2] = parts[2] + u0 * u0
         parts[3] = parts[3] + (u0 * z0 + u1 * z1)
     stacked = jnp.concatenate(parts + [jnp.zeros((LANES - 4 * levels, LANES), jnp.float32)], axis=0)
@@ -293,9 +326,8 @@
     for n in range(levels):
         sol_r, sol_u, res_r, res_u, res_z = [jnp.broadcast_to(c[n : n + 1], (8, LANES)) for c in coefs]
         for g in range(rows // 8):
-            at = pl.ds(8 * g * levels + n, 8, stride=levels)
-            x, u, z = field[at, :], image[at, :], second[at, :]
-            to = pl.ds(8 * g, 8)
+            at, to = pl.ds(PAD + n * (rows + PAD) + 8 * g, 8), pl.ds(8 * g, 8)
+            x, u, z = field[at, :], image[at, :], second[pl.ds(n * rows + 8 * g, 8), :]
             solution[n, to, :] = sol_r * x + sol_u * u
             residual[n, to, :] = (res_r * x + res_u * u) + res_z * z
         if (n + 1) % PART == 0:
@@ -317,7 +349,7 @@
     slots = (groups + 2) * HALF
     messages = call(
         functools.partial(pack_kernel, groups),
-        [f32(3, levels, LANES)] * groups,
+        [f32(HALF * levels + 8, LANES)] * groups,
         [HBM] * 5,
         [
             pltpu.VMEM((slots, levels, LANES), jnp.float32),
@@ -353,24 +385,24 @@
 
     got_b = lax.ppermute(swap_b, ("comp", "dom"), pairing(lambda d: ((d + 1) ^ 1) - 1))
     got_a = lax.ppermute(swap_a, ("comp", "dom"), pairing(lambda d: d ^ 1))
-    cube = f32(rows, levels, LANES)
-    field, outer, helm_outer, image, second, sums = call(
+    flat, padded = f32(levels * rows, LANES), f32(PAD + levels * (rows + PAD), LANES)
+    field, image, second, sums = call(
         functools.partial(inner_kernel, groups),
-        [cube, cube, f32(rows, LANES), cube, cube, f32(4, levels, LANES)],
+        [padded, padded, flat, f32(4 * levels, LANES)],
         [VMEM] * (1 + groups),
+        [pltpu.VMEM(padded.shape, padded.dtype), pltpu.VMEM(helm.shape, helm.dtype)],
         name="inner",
         flops=60 * rows * levels * LANES,
     )(helm, *arrived)
     image, second, partial = call(
         rim_kernel,
-        [cube, cube, f32(groups * doms, 1, LANES)],
-        [VMEM] * 9,
+        [padded, flat, f32(groups * doms, 1, LANES)],
+        [VMEM] * 7,
         name="rim",
-        aliases={4: 0, 5: 1},
-    )(helm, helm_outer, field, outer, image, second, sums, got_b, got_a)
+        aliases={2: 0, 3: 1},
+    )(helm, field, image, second, sums, got_b, got_a)
     partials = lax.all_to_all(partial, ("comp", "dom"), split_axis=0, concat_axis=0, tiled=True)
     whole = f32(levels, rows, LANES)
-    flat = lambda x: x.reshape(rows * levels, LANES)
     return tuple(
         call(
             final_kernel,
@@ -379,7 +411,7 @@
             [pltpu.VMEM(whole.shape, whole.dtype)] * 2 + [pltpu.SemaphoreType.DMA((2 * levels // PART,))],
             name="final",
             out_spec=HBM,
-        )(partials, flat(field), flat(image), flat(second))
+        )(partials, field, image, second)
     )
 
 

time: 26.8 us -> 26.7 us (level)
  Pallas kernels: 5.17 us -> 4.77 us
  blocking collectives: 11.2 us -> 11.5 us
    pallas_call x3, Pallas kernels: 3.86 us -> 3.51 us  [the longest x1 1.71 us: per_device(): call(functools.partial(inner_kernel, groups), [padded, padded, flat, f32(...]
    all_to_all x1, blocking collectives: 11.2 us -> 11.5 us  [per_device(): lax.all_to_all(partial, ('comp', 'dom'), split_axis=0, concat_axis=0, til...]
  transfers between devices with their start and end apart: 5 -> 5, of which waited for: 2 -> 2; matrix products, arithmetic and copies ran while one was open for 0% -> 0% of each run, Pallas kernels for 8% -> 6%
where the time goes in v5:
time: 26.7 us; the launch traced here: 26.4 us
  blocking collectives  11.5 us (43%)
  starting transfers between devices  6.36 us (24%)
  Pallas kernels  4.77 us (18%)
  waiting for transfers between devices  3.06 us (11%)
  between operations  0.67 us (3%)
    all_to_all x1, blocking collectives, per_device(): lax.all_to_all(partial, ('comp', 'dom'), split_axis=0, concat_axis=0, til...  11.5 us
    ppermute x3, starting transfers between devices, per_device(): arrived.append(lax.ppermute(message, 'comp', pairs))  3.25 us
    ppermute x3, waiting for transfers between devices, per_device(): arrived.append(lax.ppermute(message, 'comp', pairs))  3.02 us
    ppermute x1, starting transfers between devices, per_device(): got_a = lax.ppermute(swap_a, ('comp', 'dom'), pairing(lambda d: d ^ 1))  2.53 us
    pallas_call x1, Pallas kernels, per_device(): call(functools.partial(inner_kernel, groups), [padded, padded, flat, f32(...  1.71 us
    pallas_call x1, Pallas kernels, per_device(): call(functools.partial(pack_kernel, groups), [f32(HALF * levels + 8, LANE...  1.55 us
    pallas_call x1, Pallas kernels, per_device(): call(final_kernel, [whole, whole], [VMEM] * 4, [pltpu.VMEM(whole.shape, w...  1.03 us
    ppermute x1, starting transfers between devices, per_device(): lax.ppermute(swap_b, ('comp', 'dom'), pairing(lambda d: (d + 1 ^ 1) - 1))  0.57 us
  transfers between devices with their start and end apart: 5, of which 2 were waited for; matrix products, arithmetic and copies ran while one was open for 0% of the time, Pallas kernels for 6%

profile of v5, /device:TPU:0, one launch (start us, length us, event | category | flops | bytes accessed | tf_op | source)
XLA Modules:
  0.0 26.4 jit_solution(10605693062765217047)
XLA Ops:
  0.6 0.0 copy-start
  0.6 1.5 %pack.1 = (f32[40,128]{1,0:T(8,128)S(1)}, f32[40,128]{1,0:T(8,128)S(1)}, f32[40,128]{1,0:T(8,128)S(1)}, f32[40,128]{1,0:T(8,128)S(1)}) custom-call(s32[12]{0:T(128)} %bitcast.9, s32[2,12]{1,0:T(2,128)} %bitcast.8, bf16[32,16,128]{2,1,0:T(8,128)(2,1)} %bitcast.7, bf16[12,128,128]{2,1,0:T(8,128)(2,1)} %bitcast.6, f32[32,128]{1,0:T(8,128)} %helm.5), custom_call_target="tpu_custom_call" | custom-call | tf_op jit(solution)/shard_map/pack/pallas_call | solution.py:350
  2.2 3.1 %collective-permute-start = (f32[40,128]{1,0:T(8,128)S(1)}, f32[40,128]{1,0:T(8,128)S(1)}, u32[]{:S(2)}, u32[]{:S(2)}) collective-permute-start(f32[40,128]{1,0:T(8,128)S(1)} %get-tuple-element.16), channel_id=1, source_target_pairs={{0,16},{8,24},{16,0},{24,8},{1,17},{9,25},{17,1},{25,9},{2,18},{10... | collective-permute-start | bytes 61448 | tf_op jit(solution)/shard_map/ppermute | solution.py:372
  5.3 0.0 collective-permute-start.1
  5.3 0.2 collective-permute-start.2
  5.4 1.6 %collective-permute-done.rest_1_ = f32[40,128]{1,0:T(8,128)S(1)} collective-permute-done((f32[40,128]{1,0:T(8,128)S(1)}, f32[40,128]{1,0:T(8,128)S(1)}, u32[]{:S(2)}, u32[]{:S(2)}) %collective-permute-start) | collective-permute-done | bytes 20512 | tf_op jit(solution)/shard_map/ppermute | solution.py:372
  7.0 0.0 collective-permute-done.1.rest_2_
  7.0 1.4 %collective-permute-done.2.rest_3_ = f32[40,128]{1,0:T(8,128)S(1)} collective-permute-done((f32[40,128]{1,0:T(8,128)S(1)}, f32[40,128]{1,0:T(8,128)S(1)}, u32[]{:S(2)}, u32[]{:S(2)}) %collective-permute-start.2) | collective-permute-done | bytes 20512 | tf_op jit(solution)/shard_map/ppermute | solution.py:372
  8.5 0.0 copy-done
  8.5 0.2 edge.1
  8.7 0.6 %collective-permute-start.3 = (f32[40,128]{1,0:T(8,128)S(1)}, f32[40,128]{1,0:T(8,128)S(1)}, u32[]{:S(2)}, u32[]{:S(2)}) collective-permute-start(f32[40,128]{1,0:T(8,128)S(1)} %get-tuple-element.23), channel_id=1, source_target_pairs={{0,8},{1,2},{2,1},{3,4},{4,3},{5,6},{6,5},{7,15},{8,0},{9,10},{10,... | collective-permute-start | bytes 61448 | tf_op jit(solution)/shard_map/ppermute | solution.py:386
  9.3 2.5 %collective-permute-start.4 = (f32[40,128]{1,0:T(8,128)S(1)}, f32[40,128]{1,0:T(8,128)S(1)}, u32[]{:S(2)}, u32[]{:S(2)}) collective-permute-start(f32[40,128]{1,0:T(8,128)S(1)} %get-tuple-element.24), channel_id=1, source_target_pairs={{0,1},{1,0},{2,3},{3,2},{4,5},{5,4},{6,7},{7,6},{8,9},{9,8},{10,11... | collective-permute-start | bytes 61448 | tf_op jit(solution)/shard_map/ppermute | solution.py:387
  11.8 1.7 %inner.1 = (f32[648,128]{1,0:T(8,128)S(1)}, f32[648,128]{1,0:T(8,128)S(1)}, f32[512,128]{1,0:T(8,128)S(1)}, f32[64,128]{1,0:T(8,128)S(1)}) custom-call(f32[32,128]{1,0:T(8,128)S(1)} %copy-done, f32[40,128]{1,0:T(8,128)S(1)} %get-tuple-element.15.rest_0_, f32[40,128]{1,0:T(8,128)S(1)} %collective-permute-done.rest_1_, ...), custom_call_target="tpu_custom_call" | custom-call | flops 3932160 | bytes 491520 | tf_op jit(solution)/shard_map/inner/pallas_call | solution.py:389
  13.5 0.0 collective-permute-done.3.got_b
  13.5 0.0 collective-permute-done.4.got_a
  13.6 0.3 rim.1
  13.8 11.5 %all_to_all.5.partials = f32[32,1,128]{2,1,0:T(1,128)S(1)} all-to-all(f32[32,1,128]{2,1,0:T(1,128)S(1)} %get-tuple-element.25), channel_id=1, replica_groups=mesh['comp'=4,'dom'=8] {'comp','dom'}, dimensions={0} | all-to-all | bytes 32768 | tf_op jit(solution)/shard_map/all_to_all | solution.py:404
  25.4 1.0 %final.1 = (f32[16,32,128]{2,1,0:T(8,128)}, f32[16,32,128]{2,1,0:T(8,128)}) custom-call(f32[32,1,128]{2,1,0:T(1,128)S(1)} %all_to_all.5.partials, f32[648,128]{1,0:T(8,128)S(1)} %get-tuple-element.19.field, f32[648,128]{1,0:T(8,128)S(1)} %get-tuple-element.26.image, f32[512,128]{1,0:T(8,128)S(1)} %get-tuple-element.27.second), custom_call_target="tpu_custom_call" | custom-call | tf_op jit(solution)/shard_map/final/pallas_call | solution.py:407
Async XLA Ops:
  0.6 7.8 %copy-start = (f32[32,128]{1,0:T(8,128)S(1)}, f32[32,128]{1,0:T(8,128)}, u32[]{:S(2)}) copy-start(f32[32,128]{1,0:T(8,128)} %helm.5) | copy-start | bytes 49156
  2.2 4.8 %collective-permute-start = (f32[40,128]{1,0:T(8,128)S(1)}, f32[40,128]{1,0:T(8,128)S(1)}, u32[]{:S(2)}, u32[]{:S(2)}) collective-permute-start(f32[40,128]{1,0:T(8,128)S(1)} %get-tuple-element.16), channel_id=1, source_target_pairs={{0,16},{8,24},{16,0},{24,8},{1,17},{9,25},{17,1},{25,9},{2,18},{10... | collective-permute-start | bytes 61448 | tf_op jit(solution)/shard_map/ppermute | solution.py:372
  5.3 1.8 %collective-permute-start.1 = (f32[40,128]{1,0:T(8,128)S(1)}, f32[40,128]{1,0:T(8,128)S(1)}, u32[]{:S(2)}, u32[]{:S(2)}) collective-permute-start(f32[40,128]{1,0:T(8,128)S(1)} %get-tuple-element.17), channel_id=1, source_target_pairs={{0,8},{8,0},{16,24},{24,16},{1,9},{9,1},{17,25},{25,17},{2,10},{10... | collective-permute-start | bytes 61448 | tf_op jit(solution)/shard_map/ppermute | solution.py:372
  5.3 3.2 %collective-permute-start.2 = (f32[40,128]{1,0:T(8,128)S(1)}, f32[40,128]{1,0:T(8,128)S(1)}, u32[]{:S(2)}, u32[]{:S(2)}) collective-permute-start(f32[40,128]{1,0:T(8,128)S(1)} %get-tuple-element.18), channel_id=1, source_target_pairs={{0,24},{8,16},{16,8},{24,0},{1,25},{9,17},{17,9},{25,1},{2,26},{10... | collective-permute-start | bytes 61448 | tf_op jit(solution)/shard_map/ppermute | solution.py:372
  8.7 4.8 %collective-permute-start.3 = (f32[40,128]{1,0:T(8,128)S(1)}, f32[40,128]{1,0:T(8,128)S(1)}, u32[]{:S(2)}, u32[]{:S(2)}) collective-permute-start(f32[40,128]{1,0:T(8,128)S(1)} %get-tuple-element.23), channel_id=1, source_target_pairs={{0,8},{1,2},{2,1},{3,4},{4,3},{5,6},{6,5},{7,15},{8,0},{9,10},{10,... | collective-permute-start | bytes 61448 | tf_op jit(solution)/shard_map/ppermute | solution.py:386
  9.3 4.3 %collective-permute-start.4 = (f32[40,128]{1,0:T(8,128)S(1)}, f32[40,128]{1,0:T(8,128)S(1)}, u32[]{:S(2)}, u32[]{:S(2)}) collective-permute-start(f32[40,128]{1,0:T(8,128)S(1)} %get-tuple-element.24), channel_id=1, source_target_pairs={{0,1},{1,0},{2,3},{3,2},{4,5},{5,4},{6,7},{7,6},{8,9},{9,8},{10,11... | collective-permute-start | bytes 61448 | tf_op jit(solution)/shard_map/ppermute | solution.py:387

commit v6 on v5

--- a/solution.py
+++ b/solution.py
@@ -12,7 +12,7 @@
 APART = 32
 HELM = 16
 SHIFT = 4.0
-PART = 4
+PART = 8
 PAD = 8
 CHUNKS = 1
 
@@ -170,16 +170,13 @@
     messages, (swap_b, swap_a) = rest[:-2], rest[-2:]
     rows, levels = helm.shape[0], (messages[0].shape[0] - 8) // HALF
     cells, beside = unpack(messages, levels)
-    lane8 = lane_ids(8)
+    lane = lane_ids(levels)
 
     def message(edge, beyond):
         x, out = cells(edge), beside(edge)
-        image = across(helm[edge : edge + 1, :], x, out) - cells(beyond)
-        corner = out[:8]
-        for g in range(1, levels // 8):
-            turned = pltpu.roll(out[8 * g : 8 * g + 8], 2 * g, 1)
-            corner = jnp.where((lane8 == 2 * g - 1) | (lane8 == 2 * g), turned, corner)
-        return x, image, corner
+        lo, hi = left(x, out), right(x, out)
+        corner = jnp.where(lane == 0, lo, jnp.where(lane == LANES - 1, hi, 0.0))
+        return x, helm[edge : edge + 1, :] * x - ((lo + hi) + (cells(beyond) + corner))
 
     low, high = message(0, 1), message(rows - 1, rows - 2)
     even = lax.rem(lax.axis_index("dom"), 2) == 0
@@ -259,11 +256,8 @@
 def rim_kernel(helm, field, image_in, second_in, sums, got_b, got_a, image, second, partial):
     rows, levels = helm.shape[0], sums.shape[0] // 4
     pitch = rows + PAD
-    comp, comps = lax.axis_index("comp"), lax.axis_size("comp")
     dom, doms = lax.axis_index("dom"), lax.axis_size("dom")
     even = lax.rem(dom, 2) == 0
-    lane = lane_ids(levels)
-    inside = ((lane == LANES - 1) & (comp > 0)) | ((lane == 0) & (comp < comps - 1))
     parts = [sums[pl.ds(j * levels, levels), :] for j in range(4)]
     for side in range(2):
         from_b = even if side == 0 else jnp.logical_not(even)
@@ -276,14 +270,12 @@
             at = pl.ds(start, size)
             return jnp.where(there, jnp.where(from_b, got_b[at], got_a[at]), 0.0)
 
-        next_row, next_image, corner = halo(0, levels), halo(levels, levels), halo(2 * levels, 8)
-        corners = [corner] + [pltpu.roll(corner, LANES - 2 * g, 1) for g in range(1, levels // 8)]
-        next_outer = jnp.where(inside, jnp.concatenate(corners, axis=0), 0.0)
+        next_row, next_image = halo(0, levels), halo(levels, levels)
         r0, u1 = field[at0, :], image_in[at1, :]
         u0 = image_in[at0, :] - next_row
         beyond = next_image - jnp.where(there, r0, 0.0)
         h = helm[first : first + 1, :]
-        z0 = second_in[to0, :] - (across(h, next_row, next_outer) + beyond)
+        z0 = second_in[to0, :] - (across(h, next_row, 0.0) + beyond)
         z1 = second_in[to1, :] + next_row
         image[at0, :] = u0
         second[to0, :] = z0
@@ -370,7 +362,7 @@
         else:
             pairs = [(c, (c + step) % groups) for c in range(groups)]
         arrived.append(lax.ppermute(message, "comp", pairs))
-    swap = f32(2 * levels + 8, LANES)
+    swap = f32(2 * levels, LANES)
     swap_b, swap_a = call(edge_kernel, [swap, swap], [VMEM] * (1 + groups), name="edge")(helm, *arrived)
 
     def pairing(beside):

time: 26.7 us -> 26.5 us (level)
  transfers between devices with their start and end apart: 5 -> 5, of which waited for: 2 -> 2; matrix products, arithmetic and copies ran while one was open for 0% -> 0% of each run, Pallas kernels for 6% -> 7%
where the time goes in v6:
time: 26.5 us; the launch traced here: 26.2 us
  blocking collectives  11.5 us (43%)
  starting transfers between devices  6.34 us (24%)
  Pallas kernels  4.67 us (18%)
  waiting for transfers between devices  3.02 us (11%)
  between operations  0.68 us (3%)
    all_to_all x1, blocking collectives, per_device(): lax.all_to_all(partial, ('comp', 'dom'), split_axis=0, concat_axis=0, til...  11.5 us
    ppermute x3, starting transfers between devices, per_device(): arrived.append(lax.ppermute(message, 'comp', pairs))  3.25 us
    ppermute x3, waiting for transfers between devices, per_device(): arrived.append(lax.ppermute(message, 'comp', pairs))  3.02 us
    ppermute x1, starting transfers between devices, per_device(): got_a = lax.ppermute(swap_a, ('comp', 'dom'), pairing(lambda d: d ^ 1))  2.53 us
    pallas_call x1, Pallas kernels, per_device(): call(functools.partial(inner_kernel, groups), [padded, padded, flat, f32(...  1.71 us
    pallas_call x1, Pallas kernels, per_device(): call(functools.partial(pack_kernel, groups), [f32(HALF * levels + 8, LANE...  1.55 us
    pallas_call x1, Pallas kernels, per_device(): call(final_kernel, [whole, whole], [VMEM] * 4, [pltpu.VMEM(whole.shape, w...  0.98 us
    ppermute x1, starting transfers between devices, per_device(): lax.ppermute(swap_b, ('comp', 'dom'), pairing(lambda d: (d + 1 ^ 1) - 1))  0.56 us
  transfers between devices with their start and end apart: 5, of which 2 were waited for; matrix products, arithmetic and copies ran while one was open for 0% of the time, Pallas kernels for 7%

profile of v6, /device:TPU:0, one launch (start us, length us, event | category | flops | bytes accessed | tf_op | source)
XLA Modules:
  0.0 26.2 jit_solution(6947493135870734789)
XLA Ops:
  0.6 0.0 copy-start
  0.6 1.6 %pack.1 = (f32[40,128]{1,0:T(8,128)S(1)}, f32[40,128]{1,0:T(8,128)S(1)}, f32[40,128]{1,0:T(8,128)S(1)}, f32[40,128]{1,0:T(8,128)S(1)}) custom-call(s32[12]{0:T(128)} %bitcast.9, s32[2,12]{1,0:T(2,128)} %bitcast.8, bf16[32,16,128]{2,1,0:T(8,128)(2,1)} %bitcast.7, bf16[12,128,128]{2,1,0:T(8,128)(2,1)} %bitcast.6, f32[32,128]{1,0:T(8,128)} %helm.5), custom_call_target="tpu_custom_call" | custom-call | tf_op jit(solution)/shard_map/pack/pallas_call | solution.py:342
  2.2 3.1 %collective-permute-start = (f32[40,128]{1,0:T(8,128)S(1)}, f32[40,128]{1,0:T(8,128)S(1)}, u32[]{:S(2)}, u32[]{:S(2)}) collective-permute-start(f32[40,128]{1,0:T(8,128)S(1)} %get-tuple-element.16), channel_id=1, source_target_pairs={{0,16},{8,24},{16,0},{24,8},{1,17},{9,25},{17,1},{25,9},{2,18},{10... | collective-permute-start | bytes 61448 | tf_op jit(solution)/shard_map/ppermute | solution.py:364
  5.3 0.0 collective-permute-start.1
  5.3 0.2 collective-permute-start.2
  5.5 1.6 %collective-permute-done.rest_1_ = f32[40,128]{1,0:T(8,128)S(1)} collective-permute-done((f32[40,128]{1,0:T(8,128)S(1)}, f32[40,128]{1,0:T(8,128)S(1)}, u32[]{:S(2)}, u32[]{:S(2)}) %collective-permute-start) | collective-permute-done | bytes 20512 | tf_op jit(solution)/shard_map/ppermute | solution.py:364
  7.0 0.0 collective-permute-done.1.rest_2_
  7.0 1.4 %collective-permute-done.2.rest_3_ = f32[40,128]{1,0:T(8,128)S(1)} collective-permute-done((f32[40,128]{1,0:T(8,128)S(1)}, f32[40,128]{1,0:T(8,128)S(1)}, u32[]{:S(2)}, u32[]{:S(2)}) %collective-permute-start.2) | collective-permute-done | bytes 20512 | tf_op jit(solution)/shard_map/ppermute | solution.py:364
  8.5 0.0 copy-done
  8.5 0.2 edge.1
  8.7 0.6 %collective-permute-start.3 = (f32[32,128]{1,0:T(8,128)S(1)}, f32[32,128]{1,0:T(8,128)S(1)}, u32[]{:S(2)}, u32[]{:S(2)}) collective-permute-start(f32[32,128]{1,0:T(8,128)S(1)} %get-tuple-element.23), channel_id=1, source_target_pairs={{0,8},{1,2},{2,1},{3,4},{4,3},{5,6},{6,5},{7,15},{8,0},{9,10},{10,... | collective-permute-start | bytes 49160 | tf_op jit(solution)/shard_map/ppermute | solution.py:378
  9.3 2.5 %collective-permute-start.4 = (f32[32,128]{1,0:T(8,128)S(1)}, f32[32,128]{1,0:T(8,128)S(1)}, u32[]{:S(2)}, u32[]{:S(2)}) collective-permute-start(f32[32,128]{1,0:T(8,128)S(1)} %get-tuple-element.24), channel_id=1, source_target_pairs={{0,1},{1,0},{2,3},{3,2},{4,5},{5,4},{6,7},{7,6},{8,9},{9,8},{10,11... | collective-permute-start | bytes 49160 | tf_op jit(solution)/shard_map/ppermute | solution.py:379
  11.8 1.7 %inner.1 = (f32[648,128]{1,0:T(8,128)S(1)}, f32[648,128]{1,0:T(8,128)S(1)}, f32[512,128]{1,0:T(8,128)S(1)}, f32[64,128]{1,0:T(8,128)S(1)}) custom-call(f32[32,128]{1,0:T(8,128)S(1)} %copy-done, f32[40,128]{1,0:T(8,128)S(1)} %get-tuple-element.15.rest_0_, f32[40,128]{1,0:T(8,128)S(1)} %collective-permute-done.rest_1_, ...), custom_call_target="tpu_custom_call" | custom-call | flops 3932160 | bytes 491520 | tf_op jit(solution)/shard_map/inner/pallas_call | solution.py:381
  13.5 0.0 collective-permute-done.3.got_b
  13.5 0.0 collective-permute-done.4.got_a
  13.5 0.2 rim.1
  13.7 11.5 %all_to_all.5.partials = f32[32,1,128]{2,1,0:T(1,128)S(1)} all-to-all(f32[32,1,128]{2,1,0:T(1,128)S(1)} %get-tuple-element.25), channel_id=1, replica_groups=mesh['comp'=4,'dom'=8] {'comp','dom'}, dimensions={0} | all-to-all | bytes 32768 | tf_op jit(solution)/shard_map/all_to_all | solution.py:396
  25.3 1.0 %final.1 = (f32[16,32,128]{2,1,0:T(8,128)}, f32[16,32,128]{2,1,0:T(8,128)}) custom-call(f32[32,1,128]{2,1,0:T(1,128)S(1)} %all_to_all.5.partials, f32[648,128]{1,0:T(8,128)S(1)} %get-tuple-element.19.field, f32[648,128]{1,0:T(8,128)S(1)} %get-tuple-element.26.image, f32[512,128]{1,0:T(8,128)S(1)} %get-tuple-element.27.second), custom_call_target="tpu_custom_call" | custom-call | tf_op jit(solution)/shard_map/final/pallas_call | solution.py:399
Async XLA Ops:
  0.6 7.8 %copy-start = (f32[32,128]{1,0:T(8,128)S(1)}, f32[32,128]{1,0:T(8,128)}, u32[]{:S(2)}) copy-start(f32[32,128]{1,0:T(8,128)} %helm.5) | copy-start | bytes 49156
  2.2 4.8 %collective-permute-start = (f32[40,128]{1,0:T(8,128)S(1)}, f32[40,128]{1,0:T(8,128)S(1)}, u32[]{:S(2)}, u32[]{:S(2)}) collective-permute-start(f32[40,128]{1,0:T(8,128)S(1)} %get-tuple-element.16), channel_id=1, source_target_pairs={{0,16},{8,24},{16,0},{24,8},{1,17},{9,25},{17,1},{25,9},{2,18},{10... | collective-permute-start | bytes 61448 | tf_op jit(solution)/shard_map/ppermute | solution.py:364
  5.3 1.8 %collective-permute-start.1 = (f32[40,128]{1,0:T(8,128)S(1)}, f32[40,128]{1,0:T(8,128)S(1)}, u32[]{:S(2)}, u32[]{:S(2)}) collective-permute-start(f32[40,128]{1,0:T(8,128)S(1)} %get-tuple-element.17), channel_id=1, source_target_pairs={{0,8},{8,0},{16,24},{24,16},{1,9},{9,1},{17,25},{25,17},{2,10},{10... | collective-permute-start | bytes 61448 | tf_op jit(solution)/shard_map/ppermute | solution.py:364
  5.3 3.2 %collective-permute-start.2 = (f32[40,128]{1,0:T(8,128)S(1)}, f32[40,128]{1,0:T(8,128)S(1)}, u32[]{:S(2)}, u32[]{:S(2)}) collective-permute-start(f32[40,128]{1,0:T(8,128)S(1)} %get-tuple-element.18), channel_id=1, source_target_pairs={{0,24},{8,16},{16,8},{24,0},{1,25},{9,17},{17,9},{25,1},{2,26},{10... | collective-permute-start | bytes 61448 | tf_op jit(solution)/shard_map/ppermute | solution.py:364
  8.7 4.8 %collective-permute-start.3 = (f32[32,128]{1,0:T(8,128)S(1)}, f32[32,128]{1,0:T(8,128)S(1)}, u32[]{:S(2)}, u32[]{:S(2)}) collective-permute-start(f32[32,128]{1,0:T(8,128)S(1)} %get-tuple-element.23), channel_id=1, source_target_pairs={{0,8},{1,2},{2,1},{3,4},{4,3},{5,6},{6,5},{7,15},{8,0},{9,10},{10,... | collective-permute-start | bytes 49160 | tf_op jit(solution)/shard_map/ppermute | solution.py:378
  9.3 4.3 %collective-permute-start.4 = (f32[32,128]{1,0:T(8,128)S(1)}, f32[32,128]{1,0:T(8,128)S(1)}, u32[]{:S(2)}, u32[]{:S(2)}) collective-permute-start(f32[32,128]{1,0:T(8,128)S(1)} %get-tuple-element.24), channel_id=1, source_target_pairs={{0,1},{1,0},{2,3},{3,2},{4,5},{5,4},{6,7},{7,6},{8,9},{9,8},{10,11... | collective-permute-start | bytes 49160 | tf_op jit(solution)/shard_map/ppermute | solution.py:379
